TPU v7x, 128 devices: a whole 4x4x4 slice. The times are simulated.
128 devices in a mesh: dp: 8 (over z, x_hi), expert: 16 (over y, x_lo, core).
Axes of the slice: x: 4 (x_hi: 2, x_lo: 2; x = x_hi * 2 + x_lo), y: 4, z: 4, core: 2. Of those that a mesh axis runs over, the one named last changes fastest.
Arguments:
- activations: bfloat16 [16, 8192, 2048], P('expert', 'dp'), may hold values from -6 to 6
- grad_hidden: bfloat16 [16, 8192, 1536], P('expert', 'dp'), may hold values from -6 to 6
- counts: int32 [16, 8], P('expert', 'dp'), may hold values from 1 to 1024, as said below
- master: float32 [16, 2048, 1536], P('expert', 'dp'), may hold values from -0.125 to 0.125
- moment1: float32 [16, 2048, 1536], P('expert', 'dp'), may hold values from -3 to 3
- moment2: float32 [16, 2048, 1536], P('expert', 'dp'), may hold values from 0.01 to 1
- old_slot: int32 [16], replicated, may hold values from 0 to 15, each once
- new_slot: int32 [16], replicated, may hold values from 0 to 15, each once
Outputs:
- master_out: float32 [16, 2048, 1536], P('expert', 'dp')
- moment1_out: float32 [16, 2048, 1536], P('expert', 'dp')
- moment2_out: float32 [16, 2048, 1536], P('expert', 'dp')
- new_weight: bfloat16 [16, 2048, 1536], P('expert')
Inputs may be any that keep to these rules, and one draw needn't show every extreme that they name: `counts`: each entry is at most 1024, and some entry equals 1024.
All inputs are finite; a program needn't handle non-finite values.
Results may differ from a plain program's by a relative error of at most 0.0055.
Values may be sent and summed in bfloat16 or wider, within the bound.
A program may use at most 128 MiB of HBM per device.

v0:
```python
import math

import jax
import jax.numpy as jnp
from jax import lax
from jax.sharding import Mesh
from jax.sharding import PartitionSpec as P

EXPERT = ("expert_0", "expert_1", "expert_2")


beta_one = 0.9
beta_two = 0.95
learn_rate = 0.01
decay_rate = 0.1
adam_eps = 1e-08
step_number = 20


def in_blocks(value, dim, peers):
    dims = value.shape
    blocks = value.reshape(*dims[:dim], peers, dims[dim] // peers, *dims[dim + 1 :])
    return jnp.moveaxis(blocks, dim, 0)


def sent_and_summed(value, axis, dim):
    blocks = in_blocks(value, dim, lax.axis_size(axis))
    arrived = lax.all_to_all(blocks, axis, split_axis=0, concat_axis=0, tiled=True)
    return arrived.astype(jnp.float32).sum(axis=0)


def in_order(blocks, dim):
    blocks = jnp.moveaxis(blocks, 0, dim)
    dims = blocks.shape
    return blocks.reshape(*dims[:dim], dims[dim] * dims[dim + 1], *dims[dim + 2 :])


def exchange_in_order(blocks, axes, sequence):
    inside = blocks.shape[1:]
    whole = blocks.reshape(*(lax.axis_size(a) for a in axes), *inside)
    for k in sequence:
        whole = lax.all_to_all(whole, axes[k], k, k, tiled=True)
    return whole.reshape(-1, *inside)


def core_and_chips(value, groups, sequence, split_dim, concat_dim):
    peers = lax.axis_size(groups[0]) * lax.axis_size(groups[1])
    blocks = in_blocks(value, split_dim, peers)
    return in_order(exchange_in_order(blocks, groups, sequence), concat_dim)


def source_slots(old_slot, new_slot):
    slots = old_slot.shape[0]
    wanted = jnp.arange(slots, dtype=jnp.int32)
    picked = jnp.where(new_slot[None, :] == wanted[:, None], old_slot[None, :], 0)
    return jnp.sum(picked, axis=1)


def adamw(grads, master, moment1, moment2):
    first = beta_one * moment1 + (1.0 - beta_one) * grads
    second = beta_two * moment2 + (1.0 - beta_two) * grads * grads
    first_hat = first / (1.0 - beta_one**step_number)
    second_hat = second / (1.0 - beta_two**step_number)
    updated = master - learn_rate * (
        first_hat / (jnp.sqrt(second_hat) + adam_eps) + decay_rate * master
    )
    return (updated, first, second)


def on_device(activations, grad_hidden, counts, master, moment1, moment2, old_slot, new_slot):
    tokens_here = activations.shape[1]
    inputs = activations[0]
    row_index = jnp.arange(tokens_here, dtype=jnp.int32)
    cotangent = jnp.where(
        (row_index < counts[0, 0])[:, None], grad_hidden[0], jnp.zeros((), jnp.bfloat16)
    )
    grad_scale = 1.0 / math.sqrt(tokens_here * lax.axis_size("dp"))
    product = lax.dot_general(
        inputs, cotangent, (((0,), (0,)), ((), ())), preferred_element_type=jnp.float32
    )
    grads = sent_and_summed((product * grad_scale).astype(jnp.bfloat16), "dp", 0)
    updated, first, second = adamw(grads, master[0], moment1[0], moment2[0])
    weight_half = updated.astype(jnp.bfloat16)[None]
    source = source_slots(old_slot, new_slot)
    spread = core_and_chips(weight_half, (("expert_0", "expert_1"), "expert_2"), (1, 0), 1, 0)
    placed = lax.all_to_all(
        jnp.take(spread, source, axis=0), EXPERT, split_axis=0, concat_axis=1, tiled=True
    )
    moved = lax.all_gather(placed, "dp", axis=1, tiled=True)
    return (updated[None], first[None], second[None], moved)


def solution(mesh):
    finer = Mesh(
        mesh.devices.reshape(mesh.shape["dp"], 4, 2, 2), ("dp", "expert_0", "expert_1", "expert_2")
    )
    in_specs = (
        P(EXPERT, "dp", None),
        P(EXPERT, "dp", None),
        P(EXPERT, "dp"),
        P(EXPERT, "dp", None),
        P(EXPERT, "dp", None),
        P(EXPERT, "dp", None),
        P(),
        P(),
    )
    out_specs = (
        P(EXPERT, "dp", None),
        P(EXPERT, "dp", None),
        P(EXPERT, "dp", None),
        P(EXPERT, None, None),
    )
    return jax.shard_map(
        on_device, mesh=finer, in_specs=in_specs, out_specs=out_specs, check_vma=False
    )
```

profile of v0, /device:TPU:0, one launch (start us, length us, event | category | flops | bytes accessed | tf_op | source)
XLA Modules:
  0.0 260.9 jit_solution(13356812411573862050)
XLA Ops:
  7.8 9.9 %multiply_convert_fusion = bf16[1536,2048]{1,0:T(8,128)(2,1)S(1)} fusion(bf16[1,1024,2048]{2,1,0:T(8,128)(2,1)} %param.8, bf16[1,1024,1536]{2,1,0:T(8,128)(2,1)} %param.9, pred[1024]{0:T(1024)(128)(4,1)S(1)} %iota_compare_fusion.1), kind=kOutput, calls=%fused_computation.2 | convolution fusion | flops 6450315264 | bytes 13632512 | tf_op jit(solution)/shard_map/dot_general | solution.py:78
  17.7 3.1 %copy.58 = bf16[192,8,8,256]{3,2,0,1:T(8,128)(2,1)} copy(bf16[192,8,8,256]{3,2,1,0:T(8,128)(2,1)S(1)} %bitcast.31) | data formatting | bytes 12582912 | tf_op jit(solution)/shard_map/reshape | solution.py:22
  20.8 0.0 copy-start
  20.8 8.0 %all-to-all-start = ((bf16[8,256,1536]{1,2,0:T(8,128)(2,1)}), bf16[8,256,1536]{1,2,0:T(8,128)(2,1)}, u32[]{:S(2)}, u32[]{:S(2)}) async-start(bf16[8,256,1536]{1,2,0:T(8,128)(2,1)} %bitcast.30), calls=%async_computation | async-start | bytes 12582912 | tf_op jit(solution)/shard_map/all_to_all | solution.py:28
  28.8 0.0 copy-done
  28.8 0.0 copy-start.5
  28.8 1.6 copy.46
  30.4 0.0 copy-done.5
  30.4 1.6 copy.41
  32.1 3.0 %copy.44 = f32[1,256,1536]{1,2,0:T(8,128)} copy(f32[1,256,1536]{2,1,0:T(8,128)} %param.13) | data formatting | bytes 3145728 | tf_op args[5]
  35.1 67.3 %all-to-all-done = bf16[8,256,1536]{1,2,0:T(8,128)(2,1)} async-done(((bf16[8,256,1536]{1,2,0:T(8,128)(2,1)}), bf16[8,256,1536]{1,2,0:T(8,128)(2,1)}, u32[]{:S(2)}, u32[]{:S(2)}) %all-to-all-start) | async-done | bytes 6291488 | tf_op jit(solution)/shard_map/all_to_all | solution.py:28
  102.3 3.8 %convert_reduce_fusion = f32[256,1536]{0,1:T(8,128)S(1)} fusion(bf16[8,256,1536]{1,2,0:T(8,128)(2,1)} %all-to-all-done), kind=kLoop, calls=%fused_computation.1 | loop fusion | flops 5898240 | bytes 7864320 | tf_op jit(solution)/shard_map/reduce_sum | solution.py:29
  106.1 1.6 copy.48
  107.8 5.9 %multiply_subtract_fusion = (f32[1,256,1536]{1,2,0:T(8,128)}, f32[1,256,1536]{1,2,0:T(8,128)}, f32[1,256,1536]{1,2,0:T(8,128)}, f32[1,256,1536]{1,2,0:T(8,128)}, f32[1,256,1536]{1,2,0:T(8,128)}) fusion(f32[1,256,1536]{1,2,0:T(8,128)} %copy.46, f32[256,1536]{0,1:T(8,128)S(1)} %convert_reduce_fusion, f32[1,256,1536]{1,2,0:T(8,128)} %copy.41, ...), kind=kLoop, calls=%fused_computation.20 | loop fusion | flops 5898240 | bytes 14155776 | tf_op jit(solution)/shard_map/sub | solution.py:64
  113.6 3.0 %copy.49 = f32[1,256,1536]{2,1,0:T(8,128)} copy(f32[1,256,1536]{1,2,0:T(8,128)} %get-tuple-element.20) | data formatting | bytes 3145728 | tf_op jit(solution)/shard_map/mul | solution.py:61
  116.7 0.0 copy-start.4
  116.7 3.2 %copy.47 = f32[1,256,1536]{2,1,0:T(8,128)} copy(f32[1,256,1536]{1,2,0:T(8,128)} %get-tuple-element.19) | data formatting | bytes 3145728 | tf_op jit(solution)/shard_map/mul | solution.py:60
  119.8 0.0 copy-done.4
  119.8 3.0 %subtract_convert_fusion = bf16[8,2,1,16,1536]{4,3,1,0,2:T(8,128)(2,1)S(1)} fusion(f32[8,2,1,16,1536]{4,3,1,0,2:T(8,128)S(1)} %bitcast.32, f32[8,2,1,16,1536]{4,3,1,0,2:T(8,128)} %bitcast.34, f32[8,2,1,16,1536]{4,3,1,0,2:T(8,128)S(1)} %bitcast.33, f32[8,2,1,16,1536]{4,3,1,0,2:T(8,128)} %bitcast.35), kind=kLoop, calls=%fused_computation.19 | loop fusion | flops 5505024 | bytes 7077888 | tf_op jit(solution)/shard_map/convert_element_type | solution.py:83
  122.8 0.1 copy.50
  122.9 4.4 %all_to_all.27 = bf16[8,2,1,16,1536]{4,3,0,2,1:T(8,128)(2,1)S(1)} all-to-all(bf16[8,2,1,16,1536]{4,3,0,2,1:T(8,128)(2,1)S(1)} %copy.50), channel_id=1, replica_groups=mesh['dp'=8,'expert_0'=4,'expert_1'=2,'expert_2'=2] {'expert_2'}, dimensions={1} | all-to-all | bytes 1572864 | tf_op jit(solution)/shard_map/all_to_all | solution.py:42
  127.3 0.0 copy-start.6
  127.3 0.0 copy-start.7
  127.3 0.9 copy.51
  128.2 4.5 %all-to-all-start.2 = ((bf16[8,2,1,16,1536]{4,3,1,2,0:T(8,128)(2,1)}), bf16[8,2,1,16,1536]{4,3,1,2,0:T(8,128)(2,1)S(1)}, u32[]{:S(2)}, u32[]{:S(2)}) async-start(bf16[8,2,1,16,1536]{4,3,1,2,0:T(8,128)(2,1)} %copy.51), calls=%async_computation.2 | async-start | bytes 1572864 | tf_op jit(solution)/shard_map/all_to_all | solution.py:42
  132.7 0.0 all-gather.2.cloned.1.call-start
  132.7 0.0 copy-done.6
  132.8 0.0 copy-done.7
  132.8 0.1 select_reduce_fusion
  132.9 13.0 %all-to-all-done.2 = bf16[8,2,1,16,1536]{4,3,1,2,0:T(8,128)(2,1)S(1)} async-done(((bf16[8,2,1,16,1536]{4,3,1,2,0:T(8,128)(2,1)}), bf16[8,2,1,16,1536]{4,3,1,2,0:T(8,128)(2,1)S(1)}, u32[]{:S(2)}, u32[]{:S(2)}) %all-to-all-start.2) | async-done | bytes 786464 | tf_op jit(solution)/shard_map/all_to_all | solution.py:42
  145.9 0.6 gather_fusion
  146.5 0.1 broadcast_select_fusion
  146.6 0.0 copy-start.3
  146.7 17.1 %all_to_all.28 = bf16[16,16,1536]{2,1,0:T(8,128)(2,1)} all-to-all(bf16[16,16,1536]{2,1,0:T(8,128)(2,1)S(1)} %broadcast_select_fusion), channel_id=1, replica_groups=mesh['dp'=8,'expert_0'=4,'expert_1'=2,'expert_2'=2] {'expert_0','expert_..., dimensions={0} | all-to-all | bytes 1572864 | tf_op jit(solution)/shard_map/all_to_all | solution.py:86
  163.7 0.0 all-gather.2.cloned.1.call-update
  163.7 0.0 copy-done.3
  163.7 0.0 copy-start.2
  163.8 1.6 copy.52
  165.4 0.0 copy-done.2
  165.4 0.0 copy-start.1
  165.4 1.6 copy.53
  167.0 0.0 copy-done.1
  167.0 1.6 copy.54
  168.6 79.6 %all-gather.2.cloned.1.call-done = bf16[1,2048,1536]{2,1,0:T(8,128)(2,1)} async-done(((bf16[1,256,1536]{2,1,0:T(8,128)(2,1)}), bf16[1,2048,1536]{2,1,0:T(8,128)(2,1)}) %all-gather.2.cloned.1.call-update) | async-done | bytes 6291472 | tf_op jit(solution)/shard_map/all_gather | solution.py:89
  248.2 5.9 %copy.61 = bf16[1,2048,1536]{2,1,0:T(8,128)(2,1)} copy(bf16[1,2048,1536]{2,1,0:T(8,128)(2,1)} %all-gather.2.cloned.1.call-done) | data formatting | bytes 12582912
  (4 shorter events, 0.0 us)
Async XLA Ops:
  20.8 8.0 %copy-start = (f32[1,256,1536]{2,1,0:T(8,128)S(1)}, f32[1,256,1536]{2,1,0:T(8,128)}, u32[]{:S(2)}) copy-start(f32[1,256,1536]{2,1,0:T(8,128)} %param.11) | copy-start | bytes 4718596
  20.8 81.5 %all-to-all-start = ((bf16[8,256,1536]{1,2,0:T(8,128)(2,1)}), bf16[8,256,1536]{1,2,0:T(8,128)(2,1)}, u32[]{:S(2)}, u32[]{:S(2)}) async-start(bf16[8,256,1536]{1,2,0:T(8,128)(2,1)} %bitcast.30), calls=%async_computation | async-start | bytes 12582912 | tf_op jit(solution)/shard_map/all_to_all | solution.py:28
  28.8 1.6 copy-start.5
  116.7 3.2 %copy-start.4 = (f32[256,1536]{1,0:T(8,128)S(1)}, f32[256,1536]{1,0:T(8,128)}, u32[]{:S(2)}) copy-start(f32[256,1536]{1,0:T(8,128)} %copy.48) | copy-start | bytes 4718596
  127.3 5.5 %copy-start.6 = (s32[16]{0:T(128)S(1)}, s32[16]{0:T(128)}, u32[]{:S(2)}) copy-start(s32[16]{0:T(128)} %param.14) | copy-start | bytes 196
  127.3 5.5 %copy-start.7 = (s32[16]{0:T(128)S(1)}, s32[16]{0:T(128)}, u32[]{:S(2)}) copy-start(s32[16]{0:T(128)} %param.15) | copy-start | bytes 196
  128.2 17.7 %all-to-all-start.2 = ((bf16[8,2,1,16,1536]{4,3,1,2,0:T(8,128)(2,1)}), bf16[8,2,1,16,1536]{4,3,1,2,0:T(8,128)(2,1)S(1)}, u32[]{:S(2)}, u32[]{:S(2)}) async-start(bf16[8,2,1,16,1536]{4,3,1,2,0:T(8,128)(2,1)} %copy.51), calls=%async_computation.2 | async-start | bytes 1572864 | tf_op jit(solution)/shard_map/all_to_all | solution.py:42
  132.7 115.5 %all-gather.2.cloned.1.call-start = ((), (), s32[]{:S(2)}) async-start(), calls=%async_computation.4 | async-start | bytes 7077888 | tf_op jit(solution)/shard_map/all_gather | solution.py:89
  146.6 17.1 %copy-start.3 = (f32[1,256,1536]{1,2,0:T(8,128)S(1)}, f32[1,256,1536]{1,2,0:T(8,128)}, u32[]{:S(2)}) copy-start(f32[1,256,1536]{1,2,0:T(8,128)} %get-tuple-element.16) | copy-start | bytes 4718596
  163.7 1.6 copy-start.2
  165.4 1.6 copy-start.1
Sparse Core Ops, SparseCore 0:
  163.9 84.2 all-gather.1
where the time goes:
time: 261 us
  waiting for transfers between devices  160 us (61%)
  local copies, waits for them, and re-layouts  29.5 us (11%)
  blocking collectives  21.4 us (8%)
  between operations  14.8 us (6%)
  other arithmetic  13 us (5%)
  starting transfers between devices  12.6 us (5%)
  matrix products  9.85 us (4%)
    all_gather x1, waiting for transfers between devices, on_device(): moved = lax.all_gather(placed, 'dp', axis=1, tiled=True)  79.6 us
    all_to_all x1, waiting for transfers between devices, sent_and_summed(): lax.all_to_all(blocks, axis, split_axis=0, concat_axis=0, tiled=True)  67.3 us
    all_to_all x1, blocking collectives, on_device(): lax.all_to_all(jnp.take(spread, source, axis=0), EXPERT, split_axis=0, co...  17.1 us
    unnamed x23, local copies, waits for them, and re-layouts  17 us
    all_to_all x1, waiting for transfers between devices, exchange_in_order(): whole = lax.all_to_all(whole, axes[k], k, k, tiled=True)  13 us
    dot_general x1, matrix products, on_device(): lax.dot_general(inputs, cotangent, (((0,), (0,)), ((), ())), preferred_el...  9.85 us
    all_to_all x1, starting transfers between devices, sent_and_summed(): lax.all_to_all(blocks, axis, split_axis=0, concat_axis=0, tiled=True)  8.02 us
    sub x1, other arithmetic, adamw(): master - learn_rate * (first_hat / (jnp.sqrt(second_hat) + adam_eps) + de...  5.87 us
  transfers between devices with their start and end apart: 3, of which 3 were waited for; matrix products, arithmetic and copies ran while one was open for 4% of the time, Pallas kernels for 0%

commit v1 on v0

v1 whole, which is shorter than its diff:
```python
import functools
import math

import jax
import jax.numpy as jnp
from jax import lax
from jax.experimental import pallas as pl
from jax.experimental.pallas import tpu as pltpu
from jax.sharding import Mesh
from jax.sharding import PartitionSpec as P

MESH = pl.DeviceIdType.MESH
AXES = ("z", "xh", "y", "xl", "c")
EXPERT = ("y", "xl", "c")
DP = ("z", "xh")

beta_one = 0.9
beta_two = 0.95
learn_rate = 0.01
decay_rate = 0.1
adam_eps = 1e-08
step_number = 20


def source_slots(old_slot, new_slot):
    slots = old_slot.shape[0]
    wanted = jnp.arange(slots, dtype=jnp.int32)
    picked = jnp.where(new_slot[None, :] == wanted[:, None], old_slot[None, :], 0)
    return jnp.sum(picked, axis=1)


def adamw(grads, master, moment1, moment2):
    first = beta_one * moment1 + (1.0 - beta_one) * grads
    second = beta_two * moment2 + (1.0 - beta_two) * grads * grads
    first_hat = first / (1.0 - beta_one**step_number)
    second_hat = second / (1.0 - beta_two**step_number)
    updated = master - learn_rate * (
        first_hat / (jnp.sqrt(second_hat) + adam_eps) + decay_rate * master
    )
    return (updated, first, second)


class Counter:
    def __init__(self):
        self.used = 0

    def take(self):
        self.used += 1
        return self.used - 1


def copies_in_all(slots):
    chunk_a = 6 + 1 + 2 * (slots - 1) + 1 + 6
    chunk_b = 8 + 6 + 2 * (slots - 1) + 6 + 7
    return 2 * chunk_a + chunk_b


def kernel(
    sizes,
    source_ref,
    count_ref,
    act_hbm,
    grad_hbm,
    master_hbm,
    first_hbm,
    second_hbm,
    master_out,
    first_out,
    second_out,
    weight_out,
    act_raw,
    act_t,
    grad_raw,
    cot,
    states,
    outs,
    ring_send_a,
    ring_recv_a,
    cross_send_a,
    cross_recv_a,
    own_a,
    cross_send_b,
    cross_recv_b,
    ring_send_b,
    ring_recv_b,
    own_b,
    updated_w,
    spread_0,
    spread_1,
    spread_2,
    chosen,
    weight,
    load_sem,
    store_sem,
    send_sem,
    recv_sem,
):
    ny, nl, nc, rows, half_w, tokens, scale = sizes
    spread = (spread_0, spread_1, spread_2)
    slots = ny * nl * nc
    piece = rows // slots
    block = 2 * rows
    wide = 2 * half_w
    z, xh, y, xl, c = (lax.axis_index(a) for a in AXES)
    me = (y * nl + xl) * nc + c
    dp_row = (z * 2 + xh) * rows
    step = min(128, rows)

    def device(zz=None, xx=None, slot=None):
        yy, ll, cc = slot if slot is not None else (y, xl, c)
        return (z if zz is None else zz, xh if xx is None else xx, yy, ll, cc)

    z_next = lax.rem(z + 1, 4)
    z_prev = lax.rem(z + 3, 4)
    toward = (device(zz=z_next), device(zz=z_prev))
    across = device(xx=1 - xh)
    others = []
    for jy in range(ny):
        for jl in range(nl):
            for jc in range(nc):
                if jy or jl or jc:
                    slot = (lax.rem(y + jy, ny), lax.rem(xl + jl, nl), lax.rem(c + jc, nc))
                    others.append((device(slot=slot), (slot[0] * nl + slot[1]) * nc + slot[2]))

    loads = []

    def load(src, dst):
        cp = pltpu.make_async_copy(src, dst, load_sem.at[len(loads)])
        cp.start()
        loads.append(cp)
        return cp

    def load_act(rel):
        base = lax.rem(z + rel, 4) * block
        got = []
        for part, at in ((0, xh), (1, 1 - xh)):
            cols = pl.ds(pl.multiple_of(base + at * rows, rows), rows)
            got.append(load(act_hbm.at[:, cols], act_raw.at[rel, :, pl.ds(part * rows, rows)]))
        return got

    def load_grad(chunk):
        cols = pl.ds(chunk * wide, wide)
        return load(grad_hbm.at[:, cols], grad_raw.at[:, cols])

    got_grad = {0: load_grad(0)}
    got_act = {3: load_act(3), 1: load_act(1)}
    got_grad[2] = load_grad(2)
    got_grad[1] = load_grad(1)
    got_act[2] = load_act(2)
    got_act[0] = load_act(0)
    got_states = [
        load(ref, states.at[n]) for n, ref in enumerate((master_hbm, first_hbm, second_hbm))
    ]

    barrier = pltpu.get_barrier_semaphore()
    partners = [toward[0], toward[1], across] + [dev for dev, _ in others]
    for dev in partners:
        pl.semaphore_signal(barrier, inc=1, device_id=dev, device_id_type=MESH)

    live = count_ref[0]

    def mask_grad(chunk):
        got_grad[chunk].wait()
        keep = lax.broadcasted_iota(jnp.int32, (tokens, 128), 0) < live
        for j in range(wide // 128):
            cols = pl.ds(chunk * wide + j * 128, 128)
            part = grad_raw[:, cols]
            cot[:, cols] = jnp.where(keep, part, jnp.zeros_like(part))

    def turn(rel):
        for cp in got_act[rel]:
            cp.wait()

        def one(i, carry):
            at = pl.ds(pl.multiple_of(i * 128, 128), 128)
            act_t[rel, at, :] = act_raw[rel, :, at].T
            return carry

        lax.fori_loop(0, block // 128, one, 0)

    def product(rel, row0, count, col0, width, write, terms=()):
        def one(i, carry):
            at = pl.multiple_of(i * step, step)
            total = jnp.dot(
                act_t[rel, pl.ds(row0 + at, step), :],
                cot[:, pl.ds(col0, width)],
                preferred_element_type=jnp.float32,
            )
            for term in terms:
                total = total + term(at).astype(jnp.float32)
            write(at, total)
            return carry

        lax.fori_loop(0, count // step, one, 0)

    counter = Counter()
    sends = []

    def send(src, dst, dev):
        n = counter.take()
        cp = pltpu.make_async_remote_copy(
            src_ref=src,
            dst_ref=dst,
            send_sem=send_sem.at[n],
            recv_sem=recv_sem.at[n],
            device_id=dev,
            device_id_type=MESH,
        )
        cp.start()
        sends.append(cp)
        return cp

    order = ((3, 2, 1, 0), (1, 2, 3, 0))
    ring = {}

    def ring_a(chunk, s, dirs=(0, 1)):
        for dr in dirs:
            col0 = chunk * wide + dr * half_w
            rel = order[dr][s]
            terms = ()
            if s:
                ring[chunk, dr, s - 1].wait_recv()
                terms = (lambda at, dr=dr: ring_recv_a[chunk, dr, s - 1, pl.ds(at, step), :],)
            if s < 3:

                def write(at, total, dr=dr):
                    ring_send_a[chunk, dr, s, pl.ds(at, step), :] = total.astype(jnp.bfloat16)

                product(rel, 0, block, col0, half_w, write, terms)
                ring[chunk, dr, s] = send(
                    ring_send_a.at[chunk, dr, s], ring_recv_a.at[chunk, dr, s], toward[dr]
                )
            else:

                def write_far(at, total, dr=dr):
                    cross_send_a[chunk, pl.ds(at, step), pl.ds(dr * half_w, half_w)] = total.astype(
                        jnp.bfloat16
                    )

                def write_own(at, total, dr=dr):
                    own_a[chunk, pl.ds(at, step), pl.ds(dr * half_w, half_w)] = total

                far = (
                    lambda at, dr=dr: ring_recv_a[chunk, dr, s - 1, pl.ds(at + rows, step), :],
                )
                product(rel, rows, rows, col0, half_w, write_far, far)
                product(rel, 0, rows, col0, half_w, write_own, terms)
        if s == 3:
            ring[chunk, "x"] = send(cross_send_a.at[chunk], cross_recv_a.at[chunk], across)

    def cross_b(dr, s):
        rel = order[dr][s]

        def write(at, total):
            cross_send_b[dr, s, pl.ds(at, step), :] = total.astype(jnp.bfloat16)

        product(rel, rows, rows, 2 * wide + dr * half_w, half_w, write)
        ring["b", "x", dr, s] = send(cross_send_b.at[dr, s], cross_recv_b.at[dr, s], across)

    def ring_b(s):
        for dr in (0, 1):
            ring["b", "x", dr, s].wait_recv()
            terms = [lambda at, dr=dr: cross_recv_b[dr, s, pl.ds(at, step), :]]
            if s:
                ring["b", dr, s - 1].wait_recv()
                terms.append(lambda at, dr=dr: ring_recv_b[dr, s - 1, pl.ds(at, step), :])
            if s < 3:

                def write(at, total, dr=dr):
                    ring_send_b[dr, s, pl.ds(at, step), :] = total.astype(jnp.bfloat16)
            else:

                def write(at, total, dr=dr):
                    own_b[pl.ds(at, step), pl.ds(dr * half_w, half_w)] = total

            product(order[dr][s], 0, rows, 2 * wide + dr * half_w, half_w, write, terms)
            if s < 3:
                ring["b", dr, s] = send(ring_send_b.at[dr, s], ring_recv_b.at[dr, s], toward[dr])

    stores = []

    def store(src, dst):
        cp = pltpu.make_async_copy(src, dst, store_sem.at[len(stores)])
        cp.start()
        stores.append(cp)

    spreads = {}

    def update(chunk):
        if chunk < 2:
            ring[chunk, "x"].wait_recv()
        cols = pl.ds(chunk * wide, wide)
        few = min(32, rows)

        def one(i, carry):
            at = pl.ds(pl.multiple_of(i * few, few), few)
            if chunk < 2:
                total = own_a[chunk, at, :] + cross_recv_a[chunk, at, :].astype(jnp.float32)
            else:
                total = own_b[at, :]
            new, first, second = adamw(
                total * scale, states[0, at, cols], states[1, at, cols], states[2, at, cols]
            )
            outs[0, at, cols] = new
            outs[1, at, cols] = first
            outs[2, at, cols] = second
            updated_w[chunk, at, :] = new.astype(jnp.bfloat16)
            return carry

        lax.fori_loop(0, rows // few, one, 0)
        spreads[chunk] = [
            send(
                updated_w.at[chunk, pl.ds(pl.multiple_of(slot * piece, piece), piece)],
                spread[chunk].at[me],
                dev,
            )
            for dev, slot in others
        ]
        spread[chunk][me] = updated_w[chunk, pl.ds(pl.multiple_of(me * piece, piece), piece), :]
        for n, ref in enumerate((master_out, first_out, second_out)):
            store(outs.at[n, :, cols], ref.at[:, cols])

    moves = {}

    def move(chunk):
        for cp in spreads[chunk]:
            cp.wait_recv()
        cols = pl.ds(chunk * wide, wide)
        for k in range(slots):
            chosen[chunk, k] = spread[chunk][source_ref[k]]
        here = pl.ds(pl.multiple_of(dp_row + me * piece, piece), piece)
        moves[chunk] = [
            send(chosen.at[chunk, slot], weight.at[here, cols], dev) for dev, slot in others
        ]
        weight[here, cols] = chosen[chunk, me]

    def land(chunk, row0, count, col0, width):
        at = (pl.ds(row0, count), pl.ds(col0, width))
        store(weight.at[at], weight_out.at[at])

    gather = {}

    def moved(chunk):
        for cp in moves[chunk]:
            cp.wait_recv()
        here = pl.ds(pl.multiple_of(dp_row, rows), rows)
        cols = pl.ds(chunk * wide, wide)
        if chunk < 2:
            gather[chunk, "x"] = send(weight.at[here, cols], weight.at[here, cols], across)
        else:
            for dr in (0, 1):
                part = pl.ds(chunk * wide + dr * half_w, half_w)
                gather["b", dr, 0] = send(weight.at[here, part], weight.at[here, part], toward[dr])
            gather["b", "x", 0] = send(weight.at[here, cols], weight.at[here, cols], across)

    def gather_a(chunk, s):
        for dr in (0, 1):
            back = (4 - s) if dr == 0 else s
            row0 = pl.multiple_of(lax.rem(z + back, 4) * block, block)
            at = (pl.ds(row0, block), pl.ds(chunk * wide + dr * half_w, half_w))
            if s == 0:
                if dr == 0:
                    gather[chunk, "x"].wait_recv()
            else:
                gather[chunk, dr, s - 1].wait_recv()
            if s < 3:
                gather[chunk, dr, s] = send(weight.at[at], weight.at[at], toward[dr])
            store(weight.at[at], weight_out.at[at])

    def gather_b(s):
        for dr in (0, 1):
            back = (4 - s) if dr == 0 else s
            row0 = pl.multiple_of((lax.rem(z + back, 4) * 2 + xh) * rows, rows)
            at = (pl.ds(row0, rows), pl.ds(2 * wide + dr * half_w, half_w))
            gather["b", dr, s - 1].wait_recv()
            if s < 3:
                gather["b", dr, s] = send(weight.at[at], weight.at[at], toward[dr])
            gather["b", "x", dr, s] = send(weight.at[at], weight.at[at], across)

    def end_b():
        gather["b", "x", 0].wait_recv()
        for s in (1, 2, 3):
            for dr in (0, 1):
                gather["b", "x", dr, s].wait_recv()
        cols = pl.ds(2 * wide, wide)
        store(weight.at[:, cols], weight_out.at[:, cols])

    mask_grad(0)
    turn(3)
    pl.semaphore_wait(barrier, len(partners))
    ring_a(0, 0, (0,))
    turn(1)
    ring_a(0, 0, (1,))
    mask_grad(2)
    cross_b(0, 0)
    cross_b(1, 0)
    mask_grad(1)
    ring_a(1, 0)
    turn(2)
    cross_b(0, 1)
    cross_b(1, 1)
    cross_b(0, 2)
    cross_b(1, 2)
    turn(0)
    cross_b(0, 3)
    cross_b(1, 3)
    ring_b(0)
    ring_a(0, 1)
    ring_b(1)
    ring_a(0, 2)
    ring_b(2)
    ring_a(1, 1)
    ring_a(0, 3)
    for cp in got_states:
        cp.wait()
    ring_b(3)
    update(2)
    update(0)
    ring_a(1, 2)
    move(2)
    move(0)
    ring_a(1, 3)
    moved(2)
    moved(0)
    update(1)
    gather_b(1)
    gather_a(0, 0)
    move(1)
    gather_b(2)
    gather_a(0, 1)
    moved(1)
    gather_b(3)
    gather_a(1, 0)
    gather_a(0, 2)
    gather_a(1, 1)
    gather_a(0, 3)
    gather_a(1, 2)
    end_b()
    gather_a(1, 3)
    for cp in sends:
        cp.wait_send()
    for cp in stores:
        cp.wait()


def solution(mesh):
    finer = Mesh(mesh.devices.reshape(4, 2, 4, 2, 2), AXES)
    return build(finer)


def build(finer):
    ny, nl, nc = (finer.shape[a] for a in EXPERT)
    slots = ny * nl * nc

    def on_device(act, grad, counts, master, moment1, moment2, old_slot, new_slot):
        tokens, width = act.shape[1], act.shape[2]
        columns = grad.shape[2]
        rows = width // 8
        half_w = columns // 6
        wide = 2 * half_w
        block = 2 * rows
        piece = rows // slots
        bf, f32 = jnp.bfloat16, jnp.float32
        sizes = (ny, nl, nc, rows, half_w, tokens, 1.0 / math.sqrt(tokens * 8))
        any_spec = pl.BlockSpec(memory_space=pl.ANY)
        smem = pl.BlockSpec(memory_space=pltpu.SMEM)
        copies = copies_in_all(slots)
        state = jax.ShapeDtypeStruct((rows, columns), f32)
        new, first, second, moved = pl.pallas_call(
            functools.partial(kernel, sizes),
            out_shape=(state, state, state, jax.ShapeDtypeStruct((width, columns), bf)),
            in_specs=[smem, smem] + [any_spec] * 5,
            out_specs=(any_spec,) * 4,
            scratch_shapes=[
                pltpu.VMEM((4, tokens, block), bf),
                pltpu.VMEM((4, block, tokens), bf),
                pltpu.VMEM((tokens, columns), bf),
                pltpu.VMEM((tokens, columns), bf),
                pltpu.VMEM((3, rows, columns), f32),
                pltpu.VMEM((3, rows, columns), f32),
                pltpu.VMEM((2, 2, 3, block, half_w), bf),
                pltpu.VMEM((2, 2, 3, block, half_w), bf),
                pltpu.VMEM((2, rows, wide), bf),
                pltpu.VMEM((2, rows, wide), bf),
                pltpu.VMEM((2, rows, wide), f32),
                pltpu.VMEM((2, 4, rows, half_w), bf),
                pltpu.VMEM((2, 4, rows, half_w), bf),
                pltpu.VMEM((2, 3, rows, half_w), bf),
                pltpu.VMEM((2, 3, rows, half_w), bf),
                pltpu.VMEM((rows, wide), f32),
                pltpu.VMEM((3, rows, wide), bf),
                pltpu.VMEM((slots, piece, wide), bf),
                pltpu.VMEM((slots, piece, wide), bf),
                pltpu.VMEM((slots, piece, wide), bf),
                pltpu.VMEM((3, slots, piece, wide), bf),
                pltpu.VMEM((width, columns), bf),
                pltpu.SemaphoreType.DMA((14,)),
                pltpu.SemaphoreType.DMA((26,)),
                pltpu.SemaphoreType.DMA((copies,)),
                pltpu.SemaphoreType.DMA((copies,)),
            ],
            compiler_params=pltpu.CompilerParams(
                collective_id=0, has_side_effects=True, vmem_limit_bytes=60 << 20
            ),
            name="step",
        )(
            source_slots(old_slot, new_slot),
            counts[0],
            act[0],
            grad[0],
            master[0],
            moment1[0],
            moment2[0],
        )
        return (new[None], first[None], second[None], moved[None])

    in_specs = (
        P(EXPERT, DP, None),
        P(EXPERT, DP, None),
        P(EXPERT, DP),
        P(EXPERT, DP, None),
        P(EXPERT, DP, None),
        P(EXPERT, DP, None),
        P(),
        P(),
    )
    out_specs = (
        P(EXPERT, DP, None),
        P(EXPERT, DP, None),
        P(EXPERT, DP, None),
        P(EXPERT, None, None),
    )
    return jax.shard_map(on_device, mesh=finer, in_specs=in_specs, out_specs=out_specs, check_vma=False)
```

time: 261 us -> 144 us (0.55)
  waiting for transfers between devices: 160 us -> 0 us
  Pallas kernels: 0 us -> 130 us
  blocking collectives: 21.4 us -> 0 us
  local copies, waits for them, and re-layouts: 29.5 us -> 10.9 us
  between operations: 14.8 us -> 1.3 us
  starting transfers between devices: 12.6 us -> 0 us
  other arithmetic: 13 us -> 1.3 us
  matrix products: 9.85 us -> 0 us
    pallas_call x0 -> x1, Pallas kernels: none -> 130 us  [on_device(): pl.pallas_call(functools.partial(kernel, sizes), out_shape=(state, state,...]
    all_to_all x2 -> x0, waiting for transfers between devices: 80.2 us -> none  [the longest x1 67.3 us: sent_and_summed(): lax.all_to_all(blocks, axis, split_axis=0, concat_axis=0, tiled=True)]
    all_gather x1 -> x0, waiting for transfers between devices: 79.6 us -> none  [on_device(): moved = lax.all_gather(placed, 'dp', axis=1, tiled=True)]
    all_to_all x2 -> x0, blocking collectives: 21.4 us -> none  [the longest x1 17.1 us: on_device(): lax.all_to_all(jnp.take(spread, source, axis=0), EXPERT, split_axis=0, co...]
    all_to_all x2 -> x0, starting transfers between devices: 12.5 us -> none  [the longest x1 8.02 us: sent_and_summed(): lax.all_to_all(blocks, axis, split_axis=0, concat_axis=0, tiled=True)]
    dot_general x1 -> x0, matrix products: 9.85 us -> none  [on_device(): lax.dot_general(inputs, cotangent, (((0,), (0,)), ((), ())), preferred_el...]
    mul x2 -> x0, local copies, waits for them, and re-layouts: 6.19 us -> none  [the longest x1 3.15 us: adamw(): first = beta_one * moment1 + (1.0 - beta_one) * grads]
    unnamed x23 -> x6, local copies, waits for them, and re-layouts: 17 us -> 10.9 us
  transfers between devices with their start and end apart: 3 -> 0, of which waited for: 3 -> 0; matrix products, arithmetic and copies ran while one was open for 4% -> 0% of each run, Pallas kernels for 0% -> 0%
where the time goes in v1:
time: 144 us
  Pallas kernels  130 us (90%)
  local copies, waits for them, and re-layouts  10.9 us (8%)
    pallas_call x1, Pallas kernels, on_device(): pl.pallas_call(functools.partial(kernel, sizes), out_shape=(state, state,...  130 us
    unnamed x6, local copies, waits for them, and re-layouts  10.9 us

profile of v1, /device:TPU:0, one launch (start us, length us, event | category | flops | bytes accessed | tf_op | source)
XLA Modules:
  0.0 143.5 jit_solution(12723783606221868501)
XLA Ops:
  1.3 1.3 select_reduce_fusion.source_ref
  2.6 130.1 %step.1 = (f32[256,1536]{1,0:T(8,128)}, f32[256,1536]{1,0:T(8,128)}, f32[256,1536]{1,0:T(8,128)}, bf16[2048,1536]{1,0:T(8,128)(2,1)}) custom-call(s32[16]{0:T(128)} %select_reduce_fusion.source_ref, s32[1]{0:T(128)} %bitcast.10.count_ref, bf16[1024,2048]{1,0:T(8,128)(2,1)} %bitcast.12, bf16[1024,1536]{1,0:T(8,128)(2,1)} %bitcast.13, f32[256,1536]{1,0:T(8,128)} %bitcast.14, ...), custom_call_target="tpu_custom_call" | custom-call | tf_op jit(solution)/shard_map/step/pallas_call | solution.py:469
  132.6 0.0 copy-start
  132.7 2.8 %copy.17 = f32[1,256,1536]{2,1,0:T(8,128)} copy(f32[1,256,1536]{2,1,0:T(8,128)} %bitcast.19) | data formatting | bytes 3145728
  135.5 2.7 %copy.18 = f32[1,256,1536]{2,1,0:T(8,128)} copy(f32[1,256,1536]{2,1,0:T(8,128)} %bitcast.18) | data formatting | bytes 3145728
  138.2 2.7 %copy.19 = f32[1,256,1536]{2,1,0:T(8,128)} copy(f32[1,256,1536]{2,1,0:T(8,128)} %bitcast.17) | data formatting | bytes 3145728
  140.8 0.0 copy-done
  140.8 2.7 %copy.20 = bf16[1,2048,1536]{2,1,0:T(8,128)(2,1)} copy(bf16[1,2048,1536]{2,1,0:T(8,128)(2,1)S(1)} %bitcast.11) | data formatting | bytes 12582912
Async XLA Ops:
  132.6 8.2 %copy-start = (bf16[2048,1536]{1,0:T(8,128)(2,1)S(1)}, bf16[2048,1536]{1,0:T(8,128)(2,1)}, u32[]{:S(2)}) copy-start(bf16[2048,1536]{1,0:T(8,128)(2,1)} %get-tuple-element.11) | copy-start | bytes 18874372

commit v2 on v1

--- a/solution.py
+++ b/solution.py
@@ -20,13 +20,6 @@
 decay_rate = 0.1
 adam_eps = 1e-08
 step_number = 20
-
-
-def source_slots(old_slot, new_slot):
-    slots = old_slot.shape[0]
-    wanted = jnp.arange(slots, dtype=jnp.int32)
-    picked = jnp.where(new_slot[None, :] == wanted[:, None], old_slot[None, :], 0)
-    return jnp.sum(picked, axis=1)
 
 
 def adamw(grads, master, moment1, moment2):
@@ -57,7 +50,8 @@
 
 def kernel(
     sizes,
-    source_ref,
+    old_ref,
+    new_ref,
     count_ref,
     act_hbm,
     grad_hbm,
@@ -67,13 +61,12 @@
     master_out,
     first_out,
     second_out,
-    weight_out,
+    weight,
     act_raw,
     act_t,
     grad_raw,
     cot,
     states,
-    outs,
     ring_send_a,
     ring_recv_a,
     cross_send_a,
@@ -89,9 +82,8 @@
     spread_1,
     spread_2,
     chosen,
-    weight,
+    source,
     load_sem,
-    store_sem,
     send_sem,
     recv_sem,
 ):
@@ -104,7 +96,7 @@
     z, xh, y, xl, c = (lax.axis_index(a) for a in AXES)
     me = (y * nl + xl) * nc + c
     dp_row = (z * 2 + xh) * rows
-    step = min(128, rows)
+    step = min(256, rows)
 
     def device(zz=None, xx=None, slot=None):
         yy, ll, cc = slot if slot is not None else (y, xl, c)
@@ -277,13 +269,6 @@
             if s < 3:
                 ring["b", dr, s] = send(ring_send_b.at[dr, s], ring_recv_b.at[dr, s], toward[dr])
 
-    stores = []
-
-    def store(src, dst):
-        cp = pltpu.make_async_copy(src, dst, store_sem.at[len(stores)])
-        cp.start()
-        stores.append(cp)
-
     spreads = {}
 
     def update(chunk):
@@ -301,9 +286,9 @@
             new, first, second = adamw(
                 total * scale, states[0, at, cols], states[1, at, cols], states[2, at, cols]
             )
-            outs[0, at, cols] = new
-            outs[1, at, cols] = first
-            outs[2, at, cols] = second
+            master_out[at, cols] = new
+            first_out[at, cols] = first
+            second_out[at, cols] = second
             updated_w[chunk, at, :] = new.astype(jnp.bfloat16)
             return carry
 
@@ -317,8 +302,6 @@
             for dev, slot in others
         ]
         spread[chunk][me] = updated_w[chunk, pl.ds(pl.multiple_of(me * piece, piece), piece), :]
-        for n, ref in enumerate((master_out, first_out, second_out)):
-            store(outs.at[n, :, cols], ref.at[:, cols])
 
     moves = {}
 
@@ -327,16 +310,12 @@
             cp.wait_recv()
         cols = pl.ds(chunk * wide, wide)
         for k in range(slots):
-            chosen[chunk, k] = spread[chunk][source_ref[k]]
+            chosen[chunk, k] = spread[chunk][source[k]]
         here = pl.ds(pl.multiple_of(dp_row + me * piece, piece), piece)
         moves[chunk] = [
             send(chosen.at[chunk, slot], weight.at[here, cols], dev) for dev, slot in others
         ]
         weight[here, cols] = chosen[chunk, me]
-
-    def land(chunk, row0, count, col0, width):
-        at = (pl.ds(row0, count), pl.ds(col0, width))
-        store(weight.at[at], weight_out.at[at])
 
     gather = {}
 
@@ -351,7 +330,11 @@
             for dr in (0, 1):
                 part = pl.ds(chunk * wide + dr * half_w, half_w)
                 gather["b", dr, 0] = send(weight.at[here, part], weight.at[here, part], toward[dr])
-            gather["b", "x", 0] = send(weight.at[here, cols], weight.at[here, cols], across)
+
+    def back_b():
+        here = pl.ds(pl.multiple_of(dp_row, rows), rows)
+        cols = pl.ds(2 * wide, wide)
+        gather["b", "x", 0] = send(weight.at[here, cols], weight.at[here, cols], across)
 
     def gather_a(chunk, s):
         for dr in (0, 1):
@@ -365,7 +348,6 @@
                 gather[chunk, dr, s - 1].wait_recv()
             if s < 3:
                 gather[chunk, dr, s] = send(weight.at[at], weight.at[at], toward[dr])
-            store(weight.at[at], weight_out.at[at])
 
     def gather_b(s):
         for dr in (0, 1):
@@ -382,65 +364,82 @@
         for s in (1, 2, 3):
             for dr in (0, 1):
                 gather["b", "x", dr, s].wait_recv()
-        cols = pl.ds(2 * wide, wide)
-        store(weight.at[:, cols], weight_out.at[:, cols])
-
-    mask_grad(0)
-    turn(3)
-    pl.semaphore_wait(barrier, len(partners))
-    ring_a(0, 0, (0,))
-    turn(1)
-    ring_a(0, 0, (1,))
-    mask_grad(2)
-    cross_b(0, 0)
-    cross_b(1, 0)
-    mask_grad(1)
-    ring_a(1, 0)
-    turn(2)
-    cross_b(0, 1)
-    cross_b(1, 1)
-    cross_b(0, 2)
-    cross_b(1, 2)
-    turn(0)
-    cross_b(0, 3)
-    cross_b(1, 3)
-    ring_b(0)
-    ring_a(0, 1)
-    ring_b(1)
-    ring_a(0, 2)
-    ring_b(2)
-    ring_a(1, 1)
-    ring_a(0, 3)
-    for cp in got_states:
-        cp.wait()
-    ring_b(3)
-    update(2)
-    update(0)
-    ring_a(1, 2)
-    move(2)
-    move(0)
-    ring_a(1, 3)
-    moved(2)
-    moved(0)
-    update(1)
-    gather_b(1)
-    gather_a(0, 0)
-    move(1)
-    gather_b(2)
-    gather_a(0, 1)
-    moved(1)
-    gather_b(3)
-    gather_a(1, 0)
-    gather_a(0, 2)
-    gather_a(1, 1)
-    gather_a(0, 3)
-    gather_a(1, 2)
-    end_b()
-    gather_a(1, 3)
+
+    def find_sources():
+        for k in range(slots):
+            found = jnp.int32(0)
+            for e in range(slots):
+                found = jnp.where(new_ref[e] == k, old_ref[e], found)
+            source[k] = found
+
+    def enter():
+        pl.semaphore_wait(barrier, len(partners))
+
+    def ready():
+        for cp in got_states:
+            cp.wait()
+
+    plan = (
+        (find_sources,),
+        (mask_grad, 0),
+        (turn, 3),
+        (enter,),
+        (ring_a, 0, 0, (0,)),
+        (turn, 1),
+        (ring_a, 0, 0, (1,)),
+        (mask_grad, 2),
+        (cross_b, 0, 0),
+        (cross_b, 1, 0),
+        (mask_grad, 1),
+        (ring_a, 1, 0),
+        (turn, 2),
+        (cross_b, 0, 1),
+        (cross_b, 1, 1),
+        (cross_b, 0, 2),
+        (cross_b, 1, 2),
+        (ring_a, 0, 1),
+        (ring_b, 0),
+        (turn, 0),
+        (cross_b, 0, 3),
+        (cross_b, 1, 3),
+        (ring_a, 0, 2),
+        (ring_b, 1),
+        (ring_a, 1, 1),
+        (ring_a, 0, 3),
+        (ring_b, 2),
+        (ready,),
+        (ring_a, 1, 2),
+        (update, 0),
+        (ring_b, 3),
+        (update, 2),
+        (move, 0),
+        (ring_a, 1, 3),
+        (move, 2),
+        (moved, 0),
+        (moved, 2),
+        (back_b,),
+        (update, 1),
+        (gather_a, 0, 0),
+        (gather_b, 1),
+        (move, 1),
+        (gather_a, 0, 1),
+        (gather_b, 2),
+        (moved, 1),
+        (gather_a, 0, 2),
+        (gather_b, 3),
+        (gather_a, 1, 0),
+        (gather_a, 0, 3),
+        (gather_a, 1, 1),
+        (gather_a, 1, 2),
+        (end_b,),
+        (gather_a, 1, 3),
+    )
+    for task, *given in plan:
+        label = "_".join([task.__name__] + [str(g) for g in given])
+        with jax.named_scope(label):
+            task(*given)
     for cp in sends:
         cp.wait_send()
-    for cp in stores:
-        cp.wait()
 
 
 def solution(mesh):
@@ -465,18 +464,17 @@
         any_spec = pl.BlockSpec(memory_space=pl.ANY)
         smem = pl.BlockSpec(memory_space=pltpu.SMEM)
         copies = copies_in_all(slots)
-        state = jax.ShapeDtypeStruct((rows, columns), f32)
+        state = pltpu.VMEM((rows, columns), f32)
         new, first, second, moved = pl.pallas_call(
             functools.partial(kernel, sizes),
-            out_shape=(state, state, state, jax.ShapeDtypeStruct((width, columns), bf)),
-            in_specs=[smem, smem] + [any_spec] * 5,
-            out_specs=(any_spec,) * 4,
+            out_shape=(state, state, state, pltpu.VMEM((width, columns), bf)),
+            in_specs=[smem, smem, smem] + [any_spec] * 5,
+            out_specs=(pl.BlockSpec(memory_space=pltpu.VMEM),) * 4,
             scratch_shapes=[
                 pltpu.VMEM((4, tokens, block), bf),
                 pltpu.VMEM((4, block, tokens), bf),
                 pltpu.VMEM((tokens, columns), bf),
                 pltpu.VMEM((tokens, columns), bf),
-                pltpu.VMEM((3, rows, columns), f32),
                 pltpu.VMEM((3, rows, columns), f32),
                 pltpu.VMEM((2, 2, 3, block, half_w), bf),
                 pltpu.VMEM((2, 2, 3, block, half_w), bf),
@@ -493,18 +491,18 @@
                 pltpu.VMEM((slots, piece, wide), bf),
                 pltpu.VMEM((slots, piece, wide), bf),
                 pltpu.VMEM((3, slots, piece, wide), bf),
-                pltpu.VMEM((width, columns), bf),
+                pltpu.SMEM((slots,), jnp.int32),
                 pltpu.SemaphoreType.DMA((14,)),
-                pltpu.SemaphoreType.DMA((26,)),
                 pltpu.SemaphoreType.DMA((copies,)),
                 pltpu.SemaphoreType.DMA((copies,)),
             ],
             compiler_params=pltpu.CompilerParams(
-                collective_id=0, has_side_effects=True, vmem_limit_bytes=60 << 20
+                collective_id=0, has_side_effects=True, vmem_limit_bytes=46 << 20
             ),
             name="step",
         )(
-            source_slots(old_slot, new_slot),
+            old_slot,
+            new_slot,
             counts[0],
             act[0],
             grad[0],

time: 144 us -> 131 us (0.910)
  Pallas kernels: 130 us -> 124 us
  local copies, waits for them, and re-layouts: 10.9 us -> 6.13 us
    pallas_call x1, Pallas kernels: 130 us -> 124 us  [on_device(): pl.pallas_call(functools.partial(kernel, sizes), out_shape=(state, state,...]
    unnamed x6 -> x4, local copies, waits for them, and re-layouts: 10.9 us -> 6.13 us
where the time goes in v2:
time: 131 us
  Pallas kernels  124 us (95%)
  local copies, waits for them, and re-layouts  6.13 us (5%)
    pallas_call x1, Pallas kernels, on_device(): pl.pallas_call(functools.partial(kernel, sizes), out_shape=(state, state,...  124 us
    unnamed x4, local copies, waits for them, and re-layouts  6.13 us

profile of v2, /device:TPU:0, one launch (start us, length us, event | category | flops | bytes accessed | tf_op | source)
XLA Modules:
  0.0 131.4 jit_solution(11027215951826993704)
XLA Ops:
  1.3 123.9 %step.1 = (f32[256,1536]{1,0:T(8,128)S(1)}, f32[256,1536]{1,0:T(8,128)S(1)}, f32[256,1536]{1,0:T(8,128)S(1)}, bf16[2048,1536]{1,0:T(8,128)(2,1)S(1)}) custom-call(s32[16]{0:T(128)} %old_ref.1, s32[16]{0:T(128)} %new_ref.1, s32[1]{0:T(128)} %bitcast.10.count_ref, bf16[1024,2048]{1,0:T(8,128)(2,1)} %bitcast.15, bf16[1024,1536]{1,0:T(8,128)(2,1)} %bitcast.16, ...), custom_call_target="tpu_custom_call" | custom-call | tf_op jit(solution)/shard_map/step/pallas_call | solution.py:468
  125.2 1.1 copy.16
  126.4 1.1 copy.17
  127.5 1.1 copy.18
  128.7 2.7 %copy.19 = bf16[1,2048,1536]{2,1,0:T(8,128)(2,1)} copy(bf16[1,2048,1536]{2,1,0:T(8,128)(2,1)S(1)} %bitcast.11) | data formatting | bytes 12582912

commit v3 on v0

v3 whole, which is shorter than its diff:
```python
import functools
import math

import jax
import jax.numpy as jnp
from jax import lax
from jax.experimental import pallas as pl
from jax.experimental.pallas import tpu as pltpu
from jax.sharding import Mesh
from jax.sharding import PartitionSpec as P

MESH = pl.DeviceIdType.MESH
AXES = ("z", "xh", "y", "xl", "c")
EXPERT = ("y", "xl", "c")
DP = ("z", "xh")

beta_one = 0.9
beta_two = 0.95
learn_rate = 0.01
decay_rate = 0.1
adam_eps = 1e-08
step_number = 20


def adamw(grads, master, moment1, moment2):
    first = beta_one * moment1 + (1.0 - beta_one) * grads
    second = beta_two * moment2 + (1.0 - beta_two) * grads * grads
    first_hat = first / (1.0 - beta_one**step_number)
    second_hat = second / (1.0 - beta_two**step_number)
    updated = master - learn_rate * (
        first_hat / (jnp.sqrt(second_hat) + adam_eps) + decay_rate * master
    )
    return (updated, first, second)


CHUNKS = (("a", 128), ("a", 128), ("a", 128), ("a", 128), ("b", 256))

PLAN = (
    ("turn", 1),
    ("turn", 2),
    ("turn", 3),
    ("mask", 3),
    ("mask", 0),
    ("find",),
    ("mask", 1),
    ("mask", 4),
    ("enter",),
    ("xb", 4, 0, 1),
    ("ra", 3, 0, 0),
    ("ra", 1, 0, 1),
    ("xb", 4, 0, 2),
    ("xb", 4, 1, 0),
    ("ra", 0, 0, 0),
    ("xb", 4, 0, 0),
    ("ra", 0, 0, 1),
    ("xb", 4, 1, 1),
    ("turn", 0),
    ("ra", 1, 1, 1),
    ("ra", 3, 1, 0),
    ("xb", 4, 1, 3),
    ("ra", 3, 0, 1),
    ("ra", 0, 1, 0),
    ("ra", 0, 1, 1),
    ("ra", 1, 0, 0),
    ("mask", 2),
    ("ra", 3, 1, 1),
    ("ra", 0, 2, 0),
    ("ra", 1, 1, 0),
    ("xb", 4, 1, 2),
    ("ra", 3, 2, 0),
    ("ra", 0, 2, 1),
    ("xb", 4, 0, 3),
    ("ra", 3, 2, 1),
    ("rb", 4, 0, 0),
    ("ra", 1, 2, 1),
    ("ra", 0, 3, 0),
    ("ra", 1, 2, 0),
    ("ra", 0, 3, 1),
    ("ra", 3, 3, 0),
    ("rb", 4, 0, 1),
    ("ra", 3, 3, 1),
    ("up", 0),
    ("ra", 2, 0, 1),
    ("ra", 2, 0, 0),
    ("ra", 1, 3, 1),
    ("rb", 4, 1, 0),
    ("ra", 1, 3, 0),
    ("up", 3),
    ("rb", 4, 1, 1),
    ("mv", 0),
    ("ra", 2, 1, 0),
    ("ra", 2, 1, 1),
    ("up", 1),
    ("rb", 4, 2, 1),
    ("mv", 3),
    ("rb", 4, 2, 0),
    ("md", 0),
    ("ra", 2, 2, 1),
    ("ra", 2, 2, 0),
    ("md", 3),
    ("rb", 4, 3, 0),
    ("rb", 4, 3, 1),
    ("up", 4),
    ("ga", 0, 0, 0),
    ("ga", 0, 0, 1),
    ("ga", 3, 0, 0),
    ("ra", 2, 3, 1),
    ("ga", 3, 0, 1),
    ("mv", 1),
    ("ga", 0, 1, 1),
    ("mv", 4),
    ("ga", 0, 1, 0),
    ("ra", 2, 3, 0),
    ("ga", 3, 1, 0),
    ("ga", 3, 1, 1),
    ("md", 1),
    ("md", 4),
    ("ga", 3, 2, 1),
    ("up", 2),
    ("bx", 4, 0, 1),
    ("ga", 0, 2, 1),
    ("ga", 0, 2, 0),
    ("gb", 4, 1, 1),
    ("ga", 1, 0, 1),
    ("gb", 4, 1, 0),
    ("mv", 2),
    ("bx", 4, 1, 1),
    ("ga", 3, 2, 0),
    ("md", 2),
    ("gb", 4, 2, 0),
    ("ga", 1, 0, 0),
    ("gb", 4, 2, 1),
    ("bx", 4, 2, 1),
    ("ga", 0, 3, 0),
    ("bx", 4, 2, 0),
    ("ga", 2, 0, 0),
    ("bx", 4, 0, 0),
    ("ga", 3, 3, 0),
    ("gb", 4, 3, 0),
    ("ga", 2, 0, 1),
    ("ga", 1, 1, 1),
    ("ga", 1, 1, 0),
    ("ga", 2, 1, 0),
    ("bx", 4, 1, 0),
    ("ga", 2, 1, 1),
    ("ga", 0, 3, 1),
    ("bx", 4, 3, 0),
    ("ga", 1, 2, 0),
    ("ga", 1, 2, 1),
    ("ga", 2, 2, 0),
    ("gb", 4, 3, 1),
    ("bx", 4, 3, 1),
    ("ga", 2, 2, 1),
    ("ga", 3, 3, 1),
    ("ga", 2, 3, 0),
    ("ga", 1, 3, 0),
    ("ga", 1, 3, 1),
    ("ga", 2, 3, 1),
    ("end", 4),
)


class Counter:
    def __init__(self):
        self.used = 0

    def take(self):
        self.used += 1
        return self.used - 1


def copies_in_all(slots):
    moving = 2 * (slots - 1)
    return sum((16 if kind == "a" else 28) + moving for kind, _ in CHUNKS)


def scratch_of(kind, half, rows, slots):
    bf, f32 = jnp.bfloat16, jnp.float32
    block = 2 * rows if kind == "a" else rows
    crossing = 1 if kind == "a" else 4
    return [
        pltpu.VMEM((2, 3, block, half), bf),
        pltpu.VMEM((2, 3, block, half), bf),
        pltpu.VMEM((2, crossing, rows, half), bf),
        pltpu.VMEM((2, crossing, rows, half), bf),
        pltpu.VMEM((2, rows, half), f32),
        pltpu.VMEM((rows, 2 * half), bf),
        pltpu.VMEM((slots, rows // slots, 2 * half), bf),
        pltpu.VMEM((slots, rows // slots, 2 * half), bf),
    ]


PER_CHUNK = 8


def kernel(
    sizes,
    old_ref,
    new_ref,
    count_ref,
    act_hbm,
    grad_hbm,
    master_hbm,
    first_hbm,
    second_hbm,
    master_out,
    first_out,
    second_out,
    weight,
    act_raw,
    act_t,
    grad_raw,
    cot,
    states,
    source,
    load_sem,
    send_sem,
    recv_sem,
    *buffers,
):
    ny, nl, nc, rows, tokens, scale = sizes
    slots = ny * nl * nc
    piece = rows // slots
    block = 2 * rows
    z, xh, y, xl, c = (lax.axis_index(a) for a in AXES)
    me = (y * nl + xl) * nc + c
    dp_row = (z * 2 + xh) * rows
    step = min(256, rows)

    kinds, halves, starts, parts = [], [], [], []
    at_column = 0
    for k, (kind, half) in enumerate(CHUNKS):
        kinds.append(kind)
        halves.append(half)
        starts.append(at_column)
        parts.append(buffers[k * PER_CHUNK : (k + 1) * PER_CHUNK])
        at_column += 2 * half
    ring_send, ring_recv, cross_send, cross_recv, own, updated, spread, chosen = zip(*parts)

    def columns(k, dr):
        return pl.ds(starts[k] + dr * halves[k], halves[k])

    def both(k):
        return pl.ds(starts[k], 2 * halves[k])

    def device(zz=None, xx=None, slot=None):
        yy, ll, cc = slot if slot is not None else (y, xl, c)
        return (z if zz is None else zz, xh if xx is None else xx, yy, ll, cc)

    z_next = lax.rem(z + 1, 4)
    z_prev = lax.rem(z + 3, 4)
    toward = (device(zz=z_next), device(zz=z_prev))
    across = device(xx=1 - xh)
    others = []
    for jy in range(ny):
        for jl in range(nl):
            for jc in range(nc):
                if jy or jl or jc:
                    slot = (lax.rem(y + jy, ny), lax.rem(xl + jl, nl), lax.rem(c + jc, nc))
                    others.append((device(slot=slot), (slot[0] * nl + slot[1]) * nc + slot[2]))

    loads = []

    def load(src, dst):
        cp = pltpu.make_async_copy(src, dst, load_sem.at[len(loads)])
        cp.start()
        loads.append(cp)
        return cp

    got = {}
    for name, *given in PLAN:
        if name == "mask":
            cols = both(given[0])
            got[name, given[0]] = [load(grad_hbm.at[:, cols], grad_raw.at[:, cols])]
        if name == "turn":
            rel = given[0]
            base = lax.rem(z + rel, 4) * block
            got[name, rel] = []
            for part, at in ((0, xh), (1, 1 - xh)):
                cols = pl.ds(pl.multiple_of(base + at * rows, rows), rows)
                got[name, rel].append(
                    load(act_hbm.at[:, cols], act_raw.at[rel, :, pl.ds(part * rows, rows)])
                )
    got["states"] = [
        load(ref, states.at[n]) for n, ref in enumerate((master_hbm, first_hbm, second_hbm))
    ]

    def loaded(*key):
        for cp in got.pop(key if len(key) > 1 else key[0], ()):
            cp.wait()

    barrier = pltpu.get_barrier_semaphore()
    partners = [toward[0], toward[1], across] + [dev for dev, _ in others]
    for dev in partners:
        pl.semaphore_signal(barrier, inc=1, device_id=dev, device_id_type=MESH)

    live = count_ref[0]

    def find():
        for k in range(slots):
            found = jnp.int32(0)
            for e in range(slots):
                found = jnp.where(new_ref[e] == k, old_ref[e], found)
            source[k] = found

    def enter():
        pl.semaphore_wait(barrier, len(partners))

    def mask(k):
        loaded("mask", k)
        keep = lax.broadcasted_iota(jnp.int32, (tokens, 128), 0) < live
        for j in range(2 * halves[k] // 128):
            cols = pl.ds(starts[k] + j * 128, 128)
            part = grad_raw[:, cols]
            cot[:, cols] = jnp.where(keep, part, jnp.zeros_like(part))

    def turn(rel):
        loaded("turn", rel)

        def one(i, carry):
            at = pl.ds(pl.multiple_of(i * 128, 128), 128)
            act_t[rel, at, :] = act_raw[rel, :, at].T
            return carry

        lax.fori_loop(0, block // 128, one, 0)

    def product(rel, row0, count, cols, write, terms=()):
        def one(i, carry):
            at = pl.multiple_of(i * step, step)
            total = jnp.dot(
                act_t[rel, pl.ds(row0 + at, step), :],
                cot[:, cols],
                preferred_element_type=jnp.float32,
            )
            for ref, first in terms:
                total = total + ref[pl.ds(at + first, step), :].astype(jnp.float32)
            write[pl.ds(at, step), :] = total.astype(write.dtype)
            return carry

        lax.fori_loop(0, count // step, one, 0)

    counter = Counter()
    sends = []
    sent = {}

    def send(src, dst, dev):
        n = counter.take()
        cp = pltpu.make_async_remote_copy(
            src_ref=src,
            dst_ref=dst,
            send_sem=send_sem.at[n],
            recv_sem=recv_sem.at[n],
            device_id=dev,
            device_id_type=MESH,
        )
        cp.start()
        sends.append(cp)
        return cp

    order = ((3, 2, 1, 0), (1, 2, 3, 0))

    def ra(k, s, dr):
        rel, cols = order[dr][s], columns(k, dr)
        if s:
            sent["z", k, dr, s - 1].wait_recv()
            before = ring_recv[k].at[dr, s - 1]
        if s < 3:
            dst = ring_send[k].at[dr, s]
            product(rel, 0, block, cols, dst, ((before, 0),) if s else ())
            sent["z", k, dr, s] = send(dst, ring_recv[k].at[dr, s], toward[dr])
        else:
            far = cross_send[k].at[dr, 0]
            product(rel, rows, rows, cols, far, ((before, rows),))
            sent["x", k, dr] = send(far, cross_recv[k].at[dr, 0], across)
            product(rel, 0, rows, cols, own[k].at[dr], ((before, 0),))

    def xb(k, dr, s):
        far = cross_send[k].at[dr, s]
        product(order[dr][s], rows, rows, columns(k, dr), far)
        sent["x", k, dr, s] = send(far, cross_recv[k].at[dr, s], across)

    def rb(k, s, dr):
        sent["x", k, dr, s].wait_recv()
        terms = [(cross_recv[k].at[dr, s], 0)]
        if s:
            sent["z", k, dr, s - 1].wait_recv()
            terms.append((ring_recv[k].at[dr, s - 1], 0))
        dst = ring_send[k].at[dr, s] if s < 3 else own[k].at[dr]
        product(order[dr][s], 0, rows, columns(k, dr), dst, terms)
        if s < 3:
            sent["z", k, dr, s] = send(dst, ring_recv[k].at[dr, s], toward[dr])

    def up(k):
        loaded("states")
        half = halves[k]
        few = min(rows, 32 * 256 // half)
        for dr in (0, 1):
            if kinds[k] == "a":
                sent["x", k, dr].wait_recv()
            cols = columns(k, dr)

            def one(i, carry, dr=dr, cols=cols):
                at = pl.ds(pl.multiple_of(i * few, few), few)
                total = own[k][dr, at, :]
                if kinds[k] == "a":
                    total = total + cross_recv[k][dr, 0, at, :].astype(jnp.float32)
                new, first, second = adamw(
                    total * scale, states[0, at, cols], states[1, at, cols], states[2, at, cols]
                )
                master_out[at, cols] = new
                first_out[at, cols] = first
                second_out[at, cols] = second
                updated[k][at, pl.ds(dr * half, half)] = new.astype(jnp.bfloat16)
                return carry

            lax.fori_loop(0, rows // few, one, 0)
        sent["spread", k] = [
            send(
                updated[k].at[pl.ds(pl.multiple_of(slot * piece, piece), piece)],
                spread[k].at[me],
                dev,
            )
            for dev, slot in others
        ]
        spread[k][me] = updated[k][pl.ds(pl.multiple_of(me * piece, piece), piece), :]

    def mv(k):
        for cp in sent["spread", k]:
            cp.wait_recv()
        for slot in range(slots):
            chosen[k][slot] = spread[k][source[slot]]
        here = (pl.ds(pl.multiple_of(dp_row + me * piece, piece), piece), both(k))
        sent["move", k] = [send(chosen[k].at[slot], weight.at[here], dev) for dev, slot in others]
        weight[here] = chosen[k][me]

    def pass_on(at, dev):
        return send(weight.at[at], weight.at[at], dev)

    def md(k):
        for cp in sent["move", k]:
            cp.wait_recv()
        here = pl.ds(pl.multiple_of(dp_row, rows), rows)
        for dr in (0, 1):
            at = (here, columns(k, dr))
            if kinds[k] == "a":
                sent["gx", k, dr] = pass_on(at, across)
            else:
                sent["gz", k, dr, 0] = pass_on(at, toward[dr])

    def z_block(s, dr):
        return lax.rem(z + ((4 - s) if dr == 0 else s), 4)

    def ga(k, s, dr):
        row0 = pl.multiple_of(z_block(s, dr) * block, block)
        if s:
            sent["gz", k, dr, s - 1].wait_recv()
        else:
            sent["gx", k, dr].wait_recv()
        if s < 3:
            sent["gz", k, dr, s] = pass_on((pl.ds(row0, block), columns(k, dr)), toward[dr])

    def b_rows(k, s, dr):
        row0 = pl.multiple_of((z_block(s, dr) * 2 + xh) * rows, rows)
        return (pl.ds(row0, rows), columns(k, dr))

    def gb(k, s, dr):
        sent["gz", k, dr, s - 1].wait_recv()
        if s < 3:
            sent["gz", k, dr, s] = pass_on(b_rows(k, s, dr), toward[dr])

    def bx(k, s, dr):
        sent["bx", k, dr, s] = pass_on(b_rows(k, s, dr), across)

    def end(k):
        for dr in (0, 1):
            for s in range(4):
                sent["bx", k, dr, s].wait_recv()

    tasks = (find, enter, mask, turn, ra, xb, rb, up, mv, md, ga, gb, bx, end)
    named = {task.__name__: task for task in tasks}
    for name, *given in PLAN:
        with jax.named_scope("_".join([name] + [str(g) for g in given])):
            named[name](*given)
    for cp in sends:
        cp.wait_send()


def solution(mesh):
    finer = Mesh(mesh.devices.reshape(4, 2, 4, 2, 2), AXES)
    return build(finer)


def build(finer):
    ny, nl, nc = (finer.shape[a] for a in EXPERT)
    slots = ny * nl * nc

    def on_device(act, grad, counts, master, moment1, moment2, old_slot, new_slot):
        tokens, width = act.shape[1], act.shape[2]
        columns = grad.shape[2]
        rows = width // 8
        block = 2 * rows
        bf, f32 = jnp.bfloat16, jnp.float32
        sizes = (ny, nl, nc, rows, tokens, 1.0 / math.sqrt(tokens * 8))
        any_spec = pl.BlockSpec(memory_space=pl.ANY)
        smem = pl.BlockSpec(memory_space=pltpu.SMEM)
        copies = copies_in_all(slots)
        state = pltpu.VMEM((rows, columns), f32)
        scratch = [
            pltpu.VMEM((4, tokens, block), bf),
            pltpu.VMEM((4, block, tokens), bf),
            pltpu.VMEM((tokens, columns), bf),
            pltpu.VMEM((tokens, columns), bf),
            pltpu.VMEM((3, rows, columns), f32),
            pltpu.SMEM((slots,), jnp.int32),
            pltpu.SemaphoreType.DMA((len(CHUNKS) + 11,)),
            pltpu.SemaphoreType.DMA((copies,)),
            pltpu.SemaphoreType.DMA((copies,)),
        ]
        for kind, half in CHUNKS:
            scratch += scratch_of(kind, half, rows, slots)
        new, first, second, moved = pl.pallas_call(
            functools.partial(kernel, sizes),
            out_shape=(state, state, state, pltpu.VMEM((width, columns), bf)),
            in_specs=[smem, smem, smem] + [any_spec] * 5,
            out_specs=(pl.BlockSpec(memory_space=pltpu.VMEM),) * 4,
            scratch_shapes=scratch,
            compiler_params=pltpu.CompilerParams(
                collective_id=0, has_side_effects=True, vmem_limit_bytes=46 << 20
            ),
            name="step",
        )(
            old_slot,
            new_slot,
            counts[0],
            act[0],
            grad[0],
            master[0],
            moment1[0],
            moment2[0],
        )
        return (new[None], first[None], second[None], moved[None])

    in_specs = (
        P(EXPERT, DP, None),
        P(EXPERT, DP, None),
        P(EXPERT, DP),
        P(EXPERT, DP, None),
        P(EXPERT, DP, None),
        P(EXPERT, DP, None),
        P(),
        P(),
    )
    out_specs = (
        P(EXPERT, DP, None),
        P(EXPERT, DP, None),
        P(EXPERT, DP, None),
        P(EXPERT, None, None),
    )
    return jax.shard_map(on_device, mesh=finer, in_specs=in_specs, out_specs=out_specs, check_vma=False)
```

time: 261 us -> 115 us (0.44)
  waiting for transfers between devices: 160 us -> 0 us
  Pallas kernels: 0 us -> 108 us
  local copies, waits for them, and re-layouts: 29.5 us -> 6.13 us
  blocking collectives: 21.4 us -> 0 us
  between operations: 14.8 us -> 1.29 us
  other arithmetic: 13 us -> 0 us
  starting transfers between devices: 12.6 us -> 0 us
  matrix products: 9.85 us -> 0 us
    pallas_call x0 -> x1, Pallas kernels: none -> 108 us  [on_device(): pl.pallas_call(functools.partial(kernel, sizes), out_shape=(state, state,...]
    all_to_all x2 -> x0, waiting for transfers between devices: 80.2 us -> none  [the longest x1 67.3 us: sent_and_summed(): lax.all_to_all(blocks, axis, split_axis=0, concat_axis=0, tiled=True)]
    all_gather x1 -> x0, waiting for transfers between devices: 79.6 us -> none  [on_device(): moved = lax.all_gather(placed, 'dp', axis=1, tiled=True)]
    all_to_all x2 -> x0, blocking collectives: 21.4 us -> none  [the longest x1 17.1 us: on_device(): lax.all_to_all(jnp.take(spread, source, axis=0), EXPERT, split_axis=0, co...]
    all_to_all x2 -> x0, starting transfers between devices: 12.5 us -> none  [the longest x1 8.02 us: sent_and_summed(): lax.all_to_all(blocks, axis, split_axis=0, concat_axis=0, tiled=True)]
    unnamed x23 -> x4, local copies, waits for them, and re-layouts: 17 us -> 6.13 us
    dot_general x1 -> x0, matrix products: 9.85 us -> none  [on_device(): lax.dot_general(inputs, cotangent, (((0,), (0,)), ((), ())), preferred_el...]
    mul x2 -> x0, local copies, waits for them, and re-layouts: 6.19 us -> none  [the longest x1 3.15 us: adamw(): first = beta_one * moment1 + (1.0 - beta_one) * grads]
  transfers between devices with their start and end apart: 3 -> 0, of which waited for: 3 -> 0; matrix products, arithmetic and copies ran while one was open for 4% -> 0% of each run, Pallas kernels for 0% -> 0%
where the time goes in v3:
time: 115 us
  Pallas kernels  108 us (94%)
  local copies, waits for them, and re-layouts  6.13 us (5%)
  between operations  1.29 us (1%)
    pallas_call x1, Pallas kernels, on_device(): pl.pallas_call(functools.partial(kernel, sizes), out_shape=(state, state,...  108 us
    unnamed x4, local copies, waits for them, and re-layouts  6.13 us

profile of v3, /device:TPU:0, one launch (start us, length us, event | category | flops | bytes accessed | tf_op | source)
XLA Modules:
  0.0 115.0 jit_solution(16657599612459079139)
XLA Ops:
  1.3 107.5 %step.1 = (f32[256,1536]{1,0:T(8,128)S(1)}, f32[256,1536]{1,0:T(8,128)S(1)}, f32[256,1536]{1,0:T(8,128)S(1)}, bf16[2048,1536]{1,0:T(8,128)(2,1)S(1)}) custom-call(s32[16]{0:T(128)} %old_ref.1, s32[16]{0:T(128)} %new_ref.1, s32[1]{0:T(128)} %bitcast.10.count_ref, bf16[1024,2048]{1,0:T(8,128)(2,1)} %bitcast.15, bf16[1024,1536]{1,0:T(8,128)(2,1)} %bitcast.16, ...), custom_call_target="tpu_custom_call" | custom-call | tf_op jit(solution)/shard_map/step/pallas_call | solution.py:521
  108.8 1.1 copy.16
  110.0 1.1 copy.17
  111.1 1.1 copy.18
  112.3 2.7 %copy.19 = bf16[1,2048,1536]{2,1,0:T(8,128)(2,1)} copy(bf16[1,2048,1536]{2,1,0:T(8,128)(2,1)S(1)} %bitcast.11) | data formatting | bytes 12582912

commit v4 on v3

--- a/solution.py
+++ b/solution.py
@@ -36,126 +36,126 @@
 CHUNKS = (("a", 128), ("a", 128), ("a", 128), ("a", 128), ("b", 256))
 
 PLAN = (
+    ("find",),
+    ("mask", 0),
     ("turn", 1),
-    ("turn", 2),
-    ("turn", 3),
-    ("mask", 3),
-    ("mask", 0),
-    ("find",),
-    ("mask", 1),
     ("mask", 4),
     ("enter",),
+    ("xb", 4, 0, 2),
+    ("ra", 0, 0, 1),
+    ("turn", 3),
+    ("ra", 0, 0, 0),
+    ("xb", 4, 1, 0),
+    ("mask", 1),
+    ("ra", 1, 0, 1),
+    ("ra", 1, 0, 0),
+    ("xb", 4, 1, 2),
+    ("turn", 2),
+    ("ra", 0, 1, 1),
+    ("turn", 0),
+    ("ra", 0, 1, 0),
+    ("xb", 4, 0, 0),
+    ("ra", 1, 1, 1),
+    ("xb", 4, 1, 1),
+    ("ra", 1, 1, 0),
     ("xb", 4, 0, 1),
-    ("ra", 3, 0, 0),
-    ("ra", 1, 0, 1),
-    ("xb", 4, 0, 2),
-    ("xb", 4, 1, 0),
-    ("ra", 0, 0, 0),
-    ("xb", 4, 0, 0),
-    ("ra", 0, 0, 1),
-    ("xb", 4, 1, 1),
-    ("turn", 0),
-    ("ra", 1, 1, 1),
-    ("ra", 3, 1, 0),
-    ("xb", 4, 1, 3),
-    ("ra", 3, 0, 1),
-    ("ra", 0, 1, 0),
-    ("ra", 0, 1, 1),
-    ("ra", 1, 0, 0),
-    ("mask", 2),
-    ("ra", 3, 1, 1),
+    ("ra", 0, 2, 1),
     ("ra", 0, 2, 0),
-    ("ra", 1, 1, 0),
-    ("xb", 4, 1, 2),
-    ("ra", 3, 2, 0),
-    ("ra", 0, 2, 1),
-    ("xb", 4, 0, 3),
-    ("ra", 3, 2, 1),
+    ("rb", 4, 0, 1),
     ("rb", 4, 0, 0),
     ("ra", 1, 2, 1),
-    ("ra", 0, 3, 0),
     ("ra", 1, 2, 0),
     ("ra", 0, 3, 1),
-    ("ra", 3, 3, 0),
-    ("rb", 4, 0, 1),
-    ("ra", 3, 3, 1),
-    ("up", 0),
+    ("mask", 2),
+    ("ra", 0, 3, 0),
+    ("xb", 4, 0, 3),
+    ("rb", 4, 1, 1),
     ("ra", 2, 0, 1),
+    ("rb", 4, 1, 0),
     ("ra", 2, 0, 0),
     ("ra", 1, 3, 1),
-    ("rb", 4, 1, 0),
     ("ra", 1, 3, 0),
-    ("up", 3),
-    ("rb", 4, 1, 1),
+    ("up", 0),
+    ("xb", 4, 1, 3),
+    ("rb", 4, 2, 0),
+    ("mask", 3),
+    ("rb", 4, 2, 1),
+    ("ra", 3, 0, 0),
+    ("up", 1),
+    ("ra", 3, 0, 1),
+    ("ra", 2, 1, 0),
     ("mv", 0),
-    ("ra", 2, 1, 0),
     ("ra", 2, 1, 1),
-    ("up", 1),
-    ("rb", 4, 2, 1),
-    ("mv", 3),
-    ("rb", 4, 2, 0),
-    ("md", 0),
-    ("ra", 2, 2, 1),
-    ("ra", 2, 2, 0),
-    ("md", 3),
     ("rb", 4, 3, 0),
     ("rb", 4, 3, 1),
     ("up", 4),
+    ("ra", 3, 1, 0),
+    ("ra", 3, 1, 1),
+    ("md", 0),
+    ("ra", 2, 2, 0),
+    ("ra", 2, 2, 1),
+    ("mv", 1),
+    ("ra", 3, 2, 0),
+    ("mv", 4),
+    ("ra", 3, 2, 1),
+    ("ra", 2, 3, 0),
+    ("ra", 2, 3, 1),
     ("ga", 0, 0, 0),
     ("ga", 0, 0, 1),
+    ("md", 1),
+    ("ra", 3, 3, 0),
+    ("md", 4),
+    ("ra", 3, 3, 1),
+    ("ga", 0, 1, 0),
+    ("ga", 0, 1, 1),
+    ("up", 2),
+    ("gb", 4, 1, 1),
+    ("bx", 4, 1, 1),
+    ("ga", 1, 0, 0),
+    ("gb", 4, 1, 0),
+    ("up", 3),
+    ("ga", 0, 2, 0),
+    ("ga", 1, 0, 1),
+    ("mv", 2),
+    ("gb", 4, 2, 1),
+    ("bx", 4, 2, 1),
+    ("ga", 1, 1, 1),
+    ("ga", 1, 1, 0),
+    ("mv", 3),
+    ("md", 2),
+    ("ga", 0, 2, 1),
+    ("gb", 4, 3, 1),
+    ("gb", 4, 2, 0),
+    ("md", 3),
+    ("bx", 4, 2, 0),
+    ("ga", 1, 2, 0),
+    ("ga", 1, 2, 1),
+    ("ga", 2, 0, 0),
+    ("gb", 4, 3, 0),
+    ("ga", 2, 0, 1),
+    ("bx", 4, 1, 0),
+    ("ga", 3, 0, 1),
+    ("bx", 4, 3, 1),
     ("ga", 3, 0, 0),
-    ("ra", 2, 3, 1),
-    ("ga", 3, 0, 1),
-    ("mv", 1),
-    ("ga", 0, 1, 1),
-    ("mv", 4),
-    ("ga", 0, 1, 0),
-    ("ra", 2, 3, 0),
+    ("bx", 4, 0, 1),
+    ("ga", 2, 1, 1),
+    ("ga", 2, 1, 0),
     ("ga", 3, 1, 0),
     ("ga", 3, 1, 1),
-    ("md", 1),
-    ("md", 4),
+    ("bx", 4, 0, 0),
+    ("bx", 4, 3, 0),
+    ("ga", 0, 3, 0),
+    ("ga", 2, 2, 1),
+    ("ga", 2, 2, 0),
     ("ga", 3, 2, 1),
-    ("up", 2),
-    ("bx", 4, 0, 1),
-    ("ga", 0, 2, 1),
-    ("ga", 0, 2, 0),
-    ("gb", 4, 1, 1),
-    ("ga", 1, 0, 1),
-    ("gb", 4, 1, 0),
-    ("mv", 2),
-    ("bx", 4, 1, 1),
+    ("ga", 0, 3, 1),
+    ("ga", 1, 3, 1),
     ("ga", 3, 2, 0),
-    ("md", 2),
-    ("gb", 4, 2, 0),
-    ("ga", 1, 0, 0),
-    ("gb", 4, 2, 1),
-    ("bx", 4, 2, 1),
-    ("ga", 0, 3, 0),
-    ("bx", 4, 2, 0),
-    ("ga", 2, 0, 0),
-    ("bx", 4, 0, 0),
     ("ga", 3, 3, 0),
-    ("gb", 4, 3, 0),
-    ("ga", 2, 0, 1),
-    ("ga", 1, 1, 1),
-    ("ga", 1, 1, 0),
-    ("ga", 2, 1, 0),
-    ("bx", 4, 1, 0),
-    ("ga", 2, 1, 1),
-    ("ga", 0, 3, 1),
-    ("bx", 4, 3, 0),
-    ("ga", 1, 2, 0),
-    ("ga", 1, 2, 1),
-    ("ga", 2, 2, 0),
-    ("gb", 4, 3, 1),
-    ("bx", 4, 3, 1),
-    ("ga", 2, 2, 1),
+    ("ga", 1, 3, 0),
     ("ga", 3, 3, 1),
+    ("ga", 2, 3, 1),
     ("ga", 2, 3, 0),
-    ("ga", 1, 3, 0),
-    ("ga", 1, 3, 1),
-    ("ga", 2, 3, 1),
     ("end", 4),
 )
 
@@ -169,9 +169,8 @@
         return self.used - 1
 
 
-def copies_in_all(slots):
-    moving = 2 * (slots - 1)
-    return sum((16 if kind == "a" else 28) + moving for kind, _ in CHUNKS)
+def semaphores_in_all():
+    return sum(18 if kind == "a" else 30 for kind, _ in CHUNKS)
 
 
 def scratch_of(kind, half, rows, slots):
@@ -225,7 +224,6 @@
     z, xh, y, xl, c = (lax.axis_index(a) for a in AXES)
     me = (y * nl + xl) * nc + c
     dp_row = (z * 2 + xh) * rows
-    step = min(256, rows)
 
     kinds, halves, starts, parts = [], [], [], []
     at_column = 0
@@ -325,6 +323,8 @@
         lax.fori_loop(0, block // 128, one, 0)
 
     def product(rel, row0, count, cols, write, terms=()):
+        step = min(count, 256)
+
         def one(i, carry):
             at = pl.multiple_of(i * step, step)
             total = jnp.dot(
@@ -343,9 +343,8 @@
     sends = []
     sent = {}
 
-    def send(src, dst, dev):
-        n = counter.take()
-        cp = pltpu.make_async_remote_copy(
+    def copy_of(src, dst, dev, n):
+        return pltpu.make_async_remote_copy(
             src_ref=src,
             dst_ref=dst,
             send_sem=send_sem.at[n],
@@ -353,7 +352,19 @@
             device_id=dev,
             device_id_type=MESH,
         )
+
+    def send(src, dst, dev):
+        cp = copy_of(src, dst, dev, counter.take())
         cp.start()
+        sends.append(cp)
+        return cp
+
+    def send_group(pairs, pieces):
+        n = counter.take()
+        for src, dst, dev in pairs:
+            copy_of(src, dst, dev, n).start()
+        whole = pieces.at[pl.ds(0, slots - 1)]
+        cp = copy_of(whole, whole, across, n)
         sends.append(cp)
         return cp
 
@@ -414,31 +425,34 @@
                 return carry
 
             lax.fori_loop(0, rows // few, one, 0)
-        sent["spread", k] = [
-            send(
-                updated[k].at[pl.ds(pl.multiple_of(slot * piece, piece), piece)],
-                spread[k].at[me],
-                dev,
-            )
-            for dev, slot in others
-        ]
+        sent["spread", k] = send_group(
+            [
+                (
+                    updated[k].at[pl.ds(pl.multiple_of(slot * piece, piece), piece)],
+                    spread[k].at[me],
+                    dev,
+                )
+                for dev, slot in others
+            ],
+            spread[k],
+        )
         spread[k][me] = updated[k][pl.ds(pl.multiple_of(me * piece, piece), piece), :]
 
     def mv(k):
-        for cp in sent["spread", k]:
-            cp.wait_recv()
+        sent["spread", k].wait_recv()
         for slot in range(slots):
             chosen[k][slot] = spread[k][source[slot]]
         here = (pl.ds(pl.multiple_of(dp_row + me * piece, piece), piece), both(k))
-        sent["move", k] = [send(chosen[k].at[slot], weight.at[here], dev) for dev, slot in others]
+        sent["move", k] = send_group(
+            [(chosen[k].at[slot], weight.at[here], dev) for dev, slot in others], chosen[k]
+        )
         weight[here] = chosen[k][me]
 
     def pass_on(at, dev):
         return send(weight.at[at], weight.at[at], dev)
 
     def md(k):
-        for cp in sent["move", k]:
-            cp.wait_recv()
+        sent["move", k].wait_recv()
         here = pl.ds(pl.multiple_of(dp_row, rows), rows)
         for dr in (0, 1):
             at = (here, columns(k, dr))
@@ -478,11 +492,33 @@
 
     tasks = (find, enter, mask, turn, ra, xb, rb, up, mv, md, ga, gb, bx, end)
     named = {task.__name__: task for task in tasks}
+    ended, issued = 0, []
     for name, *given in PLAN:
         with jax.named_scope("_".join([name] + [str(g) for g in given])):
+            if name in ("ga", "gb", "md") and len(issued) > 20:
+                until = min(issued[-20], ended + 9)
+                for cp in sends[ended:until]:
+                    cp.wait_send()
+                ended = max(ended, until)
             named[name](*given)
-    for cp in sends:
-        cp.wait_send()
+        issued.append(len(sends))
+    with jax.named_scope("rest"):
+        for cp in sends[ended:]:
+            cp.wait_send()
+
+
+def keep(*refs):
+    sem = refs[8]
+    copies = []
+    for src, dst in zip(refs[:4], refs[4:8]):
+        half = src.shape[0] // 2
+        for row0 in (0, half):
+            at = pl.ds(row0, half)
+            copies.append(pltpu.make_async_copy(src.at[at], dst.at[at], sem.at[len(copies)]))
+    for cp in copies:
+        cp.start()
+    for cp in copies:
+        cp.wait()
 
 
 def solution(mesh):
@@ -503,7 +539,7 @@
         sizes = (ny, nl, nc, rows, tokens, 1.0 / math.sqrt(tokens * 8))
         any_spec = pl.BlockSpec(memory_space=pl.ANY)
         smem = pl.BlockSpec(memory_space=pltpu.SMEM)
-        copies = copies_in_all(slots)
+        copies = semaphores_in_all()
         state = pltpu.VMEM((rows, columns), f32)
         scratch = [
             pltpu.VMEM((4, tokens, block), bf),
@@ -518,7 +554,7 @@
         ]
         for kind, half in CHUNKS:
             scratch += scratch_of(kind, half, rows, slots)
-        new, first, second, moved = pl.pallas_call(
+        results = pl.pallas_call(
             functools.partial(kernel, sizes),
             out_shape=(state, state, state, pltpu.VMEM((width, columns), bf)),
             in_specs=[smem, smem, smem] + [any_spec] * 5,
@@ -538,6 +574,15 @@
             moment1[0],
             moment2[0],
         )
+        new, first, second, moved = pl.pallas_call(
+            keep,
+            out_shape=tuple(jax.ShapeDtypeStruct(r.shape, r.dtype) for r in results),
+            in_specs=[pl.BlockSpec(memory_space=pltpu.VMEM)] * 4,
+            out_specs=(any_spec,) * 4,
+            scratch_shapes=[pltpu.SemaphoreType.DMA((8,))],
+            compiler_params=pltpu.CompilerParams(vmem_limit_bytes=1 << 20),
+            name="keep",
+        )(*results)
         return (new[None], first[None], second[None], moved[None])
 
     in_specs = (

time: 115 us -> 107 us (0.930)
  local copies, waits for them, and re-layouts: 6.13 us -> 0 us
  Pallas kernels: 108 us -> 105 us
    pallas_call x1, Pallas kernels: 108 us -> 101 us  [on_device(): pl.pallas_call(functools.partial(kernel, sizes), out_shape=(state, state,...]
    unnamed x4 -> x0, local copies, waits for them, and re-layouts: 6.13 us -> none
    pallas_call x0 -> x1, Pallas kernels: none -> 4.24 us  [on_device(): pl.pallas_call(keep, out_shape=tuple((jax.ShapeDtypeStruct(r.shape, r.dty...]
where the time goes in v4:
time: 107 us
  Pallas kernels  105 us (98%)
  between operations  1.45 us (1%)
    pallas_call x1, Pallas kernels, on_device(): pl.pallas_call(functools.partial(kernel, sizes), out_shape=(state, state,...  101 us
    pallas_call x1, Pallas kernels, on_device(): pl.pallas_call(keep, out_shape=tuple((jax.ShapeDtypeStruct(r.shape, r.dty...  4.24 us

profile of v4, /device:TPU:0, one launch (start us, length us, event | category | flops | bytes accessed | tf_op | source)
XLA Modules:
  0.0 106.7 jit_solution(15633300935105983554)
XLA Ops:
  1.3 101.0 %step.1 = (f32[256,1536]{1,0:T(8,128)S(1)}, f32[256,1536]{1,0:T(8,128)S(1)}, f32[256,1536]{1,0:T(8,128)S(1)}, bf16[2048,1536]{1,0:T(8,128)(2,1)S(1)}) custom-call(s32[16]{0:T(128)} %old_ref.1, s32[16]{0:T(128)} %new_ref.1, s32[1]{0:T(128)} %bitcast.10.count_ref, bf16[1024,2048]{1,0:T(8,128)(2,1)} %bitcast.11, bf16[1024,1536]{1,0:T(8,128)(2,1)} %bitcast.12, ...), custom_call_target="tpu_custom_call" | custom-call | tf_op jit(solution)/shard_map/step/pallas_call | solution.py:557
  102.3 4.2 %keep.1 = (f32[256,1536]{1,0:T(8,128)}, f32[256,1536]{1,0:T(8,128)}, f32[256,1536]{1,0:T(8,128)}, bf16[2048,1536]{1,0:T(8,128)(2,1)}) custom-call(f32[256,1536]{1,0:T(8,128)S(1)} %get-tuple-element.12.refs_0_, f32[256,1536]{1,0:T(8,128)S(1)} %get-tuple-element.13.refs_1_, f32[256,1536]{1,0:T(8,128)S(1)} %get-tuple-element.14.refs_2_, ...), custom_call_target="tpu_custom_call" | custom-call | tf_op jit(solution)/shard_map/keep/pallas_call | solution.py:577

commit v5 on v4

--- a/solution.py
+++ b/solution.py
@@ -36,126 +36,126 @@
 CHUNKS = (("a", 128), ("a", 128), ("a", 128), ("a", 128), ("b", 256))
 
 PLAN = (
-    ("find",),
-    ("mask", 0),
-    ("turn", 1),
+    ("turn", 3),
     ("mask", 4),
     ("enter",),
-    ("xb", 4, 0, 2),
-    ("ra", 0, 0, 1),
-    ("turn", 3),
-    ("ra", 0, 0, 0),
+    ("xb", 4, 0, 0),
+    ("mask", 3),
+    ("turn", 1),
+    ("ra", 3, 0, 1),
+    ("ra", 3, 0, 0),
     ("xb", 4, 1, 0),
     ("mask", 1),
     ("ra", 1, 0, 1),
     ("ra", 1, 0, 0),
     ("xb", 4, 1, 2),
     ("turn", 2),
-    ("ra", 0, 1, 1),
+    ("xb", 4, 1, 1),
+    ("ra", 3, 1, 1),
+    ("ra", 3, 1, 0),
     ("turn", 0),
-    ("ra", 0, 1, 0),
-    ("xb", 4, 0, 0),
+    ("rb", 4, 0, 1),
+    ("xb", 4, 0, 1),
+    ("find",),
+    ("rb", 4, 0, 0),
+    ("xb", 4, 1, 3),
+    ("ra", 3, 2, 1),
+    ("ra", 3, 2, 0),
+    ("mask", 2),
     ("ra", 1, 1, 1),
-    ("xb", 4, 1, 1),
     ("ra", 1, 1, 0),
-    ("xb", 4, 0, 1),
-    ("ra", 0, 2, 1),
-    ("ra", 0, 2, 0),
-    ("rb", 4, 0, 1),
-    ("rb", 4, 0, 0),
+    ("xb", 4, 0, 2),
+    ("rb", 4, 1, 1),
+    ("rb", 4, 1, 0),
+    ("mask", 0),
+    ("ra", 3, 3, 1),
+    ("ra", 3, 3, 0),
+    ("ra", 2, 0, 1),
     ("ra", 1, 2, 1),
     ("ra", 1, 2, 0),
-    ("ra", 0, 3, 1),
-    ("mask", 2),
-    ("ra", 0, 3, 0),
     ("xb", 4, 0, 3),
-    ("rb", 4, 1, 1),
-    ("ra", 2, 0, 1),
-    ("rb", 4, 1, 0),
+    ("rb", 4, 2, 1),
+    ("ra", 0, 0, 1),
+    ("rb", 4, 2, 0),
+    ("up", 3),
+    ("ra", 2, 1, 1),
+    ("ra", 0, 0, 0),
+    ("ra", 1, 3, 0),
+    ("ra", 1, 3, 1),
     ("ra", 2, 0, 0),
-    ("ra", 1, 3, 1),
-    ("ra", 1, 3, 0),
-    ("up", 0),
-    ("xb", 4, 1, 3),
-    ("rb", 4, 2, 0),
-    ("mask", 3),
-    ("rb", 4, 2, 1),
-    ("ra", 3, 0, 0),
-    ("up", 1),
-    ("ra", 3, 0, 1),
-    ("ra", 2, 1, 0),
-    ("mv", 0),
-    ("ra", 2, 1, 1),
     ("rb", 4, 3, 0),
+    ("mv", 3),
     ("rb", 4, 3, 1),
     ("up", 4),
-    ("ra", 3, 1, 0),
-    ("ra", 3, 1, 1),
-    ("md", 0),
+    ("ra", 0, 1, 0),
+    ("ra", 0, 1, 1),
+    ("up", 1),
+    ("ra", 2, 1, 0),
+    ("md", 3),
+    ("ra", 2, 2, 1),
+    ("ra", 0, 2, 0),
+    ("mv", 4),
+    ("ra", 0, 2, 1),
+    ("mv", 1),
     ("ra", 2, 2, 0),
-    ("ra", 2, 2, 1),
-    ("mv", 1),
-    ("ra", 3, 2, 0),
-    ("mv", 4),
-    ("ra", 3, 2, 1),
+    ("ga", 3, 0, 1),
+    ("ra", 2, 3, 1),
+    ("ga", 3, 0, 0),
+    ("ra", 0, 3, 0),
+    ("ra", 0, 3, 1),
     ("ra", 2, 3, 0),
-    ("ra", 2, 3, 1),
-    ("ga", 0, 0, 0),
-    ("ga", 0, 0, 1),
+    ("md", 4),
     ("md", 1),
-    ("ra", 3, 3, 0),
-    ("md", 4),
-    ("ra", 3, 3, 1),
-    ("ga", 0, 1, 0),
-    ("ga", 0, 1, 1),
+    ("ga", 3, 1, 0),
+    ("ga", 3, 1, 1),
+    ("up", 0),
+    ("gb", 4, 1, 0),
+    ("gb", 4, 1, 1),
     ("up", 2),
-    ("gb", 4, 1, 1),
     ("bx", 4, 1, 1),
     ("ga", 1, 0, 0),
-    ("gb", 4, 1, 0),
-    ("up", 3),
-    ("ga", 0, 2, 0),
     ("ga", 1, 0, 1),
+    ("mv", 0),
     ("mv", 2),
     ("gb", 4, 2, 1),
-    ("bx", 4, 2, 1),
+    ("ga", 3, 2, 0),
+    ("bx", 4, 0, 0),
     ("ga", 1, 1, 1),
     ("ga", 1, 1, 0),
-    ("mv", 3),
+    ("md", 0),
+    ("gb", 4, 2, 0),
+    ("gb", 4, 3, 1),
+    ("ga", 3, 2, 1),
     ("md", 2),
+    ("bx", 4, 1, 0),
+    ("ga", 1, 2, 1),
+    ("ga", 1, 2, 0),
+    ("bx", 4, 2, 1),
+    ("ga", 3, 3, 0),
+    ("ga", 0, 0, 1),
+    ("gb", 4, 3, 0),
+    ("bx", 4, 0, 1),
+    ("bx", 4, 3, 0),
+    ("ga", 0, 0, 0),
+    ("bx", 4, 3, 1),
+    ("ga", 2, 0, 0),
+    ("ga", 2, 0, 1),
+    ("ga", 0, 1, 1),
+    ("ga", 0, 1, 0),
+    ("ga", 2, 1, 0),
+    ("ga", 2, 1, 1),
     ("ga", 0, 2, 1),
-    ("gb", 4, 3, 1),
-    ("gb", 4, 2, 0),
-    ("md", 3),
+    ("ga", 0, 2, 0),
+    ("ga", 1, 3, 0),
     ("bx", 4, 2, 0),
-    ("ga", 1, 2, 0),
-    ("ga", 1, 2, 1),
-    ("ga", 2, 0, 0),
-    ("gb", 4, 3, 0),
-    ("ga", 2, 0, 1),
-    ("bx", 4, 1, 0),
-    ("ga", 3, 0, 1),
-    ("bx", 4, 3, 1),
-    ("ga", 3, 0, 0),
-    ("bx", 4, 0, 1),
-    ("ga", 2, 1, 1),
-    ("ga", 2, 1, 0),
-    ("ga", 3, 1, 0),
-    ("ga", 3, 1, 1),
-    ("bx", 4, 0, 0),
-    ("bx", 4, 3, 0),
-    ("ga", 0, 3, 0),
     ("ga", 2, 2, 1),
     ("ga", 2, 2, 0),
-    ("ga", 3, 2, 1),
+    ("ga", 2, 3, 0),
     ("ga", 0, 3, 1),
+    ("ga", 0, 3, 0),
     ("ga", 1, 3, 1),
-    ("ga", 3, 2, 0),
-    ("ga", 3, 3, 0),
-    ("ga", 1, 3, 0),
+    ("ga", 2, 3, 1),
     ("ga", 3, 3, 1),
-    ("ga", 2, 3, 1),
-    ("ga", 2, 3, 0),
     ("end", 4),
 )
 
@@ -266,26 +266,38 @@
         return cp
 
     got = {}
-    for name, *given in PLAN:
-        if name == "mask":
-            cols = both(given[0])
-            got[name, given[0]] = [load(grad_hbm.at[:, cols], grad_raw.at[:, cols])]
-        if name == "turn":
-            rel = given[0]
+    to_load = [tuple(task) for task in PLAN if task[0] in ("mask", "turn")] + [("states",)]
+
+    def load_next():
+        if not to_load:
+            return
+        key = to_load.pop(0)
+        got[key] = []
+        if key[0] == "mask":
+            cols = both(key[1])
+            got[key].append(load(grad_hbm.at[:, cols], grad_raw.at[:, cols]))
+        elif key[0] == "turn":
+            rel = key[1]
             base = lax.rem(z + rel, 4) * block
-            got[name, rel] = []
             for part, at in ((0, xh), (1, 1 - xh)):
                 cols = pl.ds(pl.multiple_of(base + at * rows, rows), rows)
-                got[name, rel].append(
+                got[key].append(
                     load(act_hbm.at[:, cols], act_raw.at[rel, :, pl.ds(part * rows, rows)])
                 )
-    got["states"] = [
-        load(ref, states.at[n]) for n, ref in enumerate((master_hbm, first_hbm, second_hbm))
-    ]
+        else:
+            for n, ref in enumerate((master_hbm, first_hbm, second_hbm)):
+                got[key].append(load(ref, states.at[n]))
+
+    for _ in range(3):
+        load_next()
 
     def loaded(*key):
-        for cp in got.pop(key if len(key) > 1 else key[0], ()):
-            cp.wait()
+        if key in got or key in to_load:
+            while key not in got:
+                load_next()
+            for cp in got.pop(key):
+                cp.wait()
+            load_next()
 
     barrier = pltpu.get_barrier_semaphore()
     partners = [toward[0], toward[1], across] + [dev for dev, _ in others]
@@ -339,32 +351,39 @@
 
         lax.fori_loop(0, count // step, one, 0)
 
-    counter = Counter()
+    counter, group_counter = Counter(), Counter()
     sends = []
     sent = {}
 
-    def copy_of(src, dst, dev, n):
+    def copy_of(src, dst, dev, n, group):
         return pltpu.make_async_remote_copy(
             src_ref=src,
             dst_ref=dst,
-            send_sem=send_sem.at[n],
+            send_sem=send_sem.at[group],
             recv_sem=recv_sem.at[n],
             device_id=dev,
             device_id_type=MESH,
         )
 
-    def send(src, dst, dev):
-        cp = copy_of(src, dst, dev, counter.take())
+    groups = {}
+
+    def send(src, dst, dev, group, size, whole):
+        if group not in groups:
+            groups[group] = [group_counter.take(), size]
+        n, left = groups[group]
+        cp = copy_of(src, dst, dev, counter.take(), n)
         cp.start()
-        sends.append(cp)
+        groups[group][1] = left - 1
+        if left == 1:
+            sends.append(copy_of(whole, whole, across, 0, n))
         return cp
 
     def send_group(pairs, pieces):
-        n = counter.take()
+        n, group = counter.take(), group_counter.take()
         for src, dst, dev in pairs:
-            copy_of(src, dst, dev, n).start()
+            copy_of(src, dst, dev, n, group).start()
         whole = pieces.at[pl.ds(0, slots - 1)]
-        cp = copy_of(whole, whole, across, n)
+        cp = copy_of(whole, whole, across, n, group)
         sends.append(cp)
         return cp
 
@@ -378,17 +397,23 @@
         if s < 3:
             dst = ring_send[k].at[dr, s]
             product(rel, 0, block, cols, dst, ((before, 0),) if s else ())
-            sent["z", k, dr, s] = send(dst, ring_recv[k].at[dr, s], toward[dr])
+            sent["z", k, dr, s] = send(
+                dst, ring_recv[k].at[dr, s], toward[dr], ("z", k), 6, ring_send[k]
+            )
         else:
             far = cross_send[k].at[dr, 0]
             product(rel, rows, rows, cols, far, ((before, rows),))
-            sent["x", k, dr] = send(far, cross_recv[k].at[dr, 0], across)
+            sent["x", k, dr] = send(
+                far, cross_recv[k].at[dr, 0], across, ("x", k), 2, cross_send[k]
+            )
             product(rel, 0, rows, cols, own[k].at[dr], ((before, 0),))
 
     def xb(k, dr, s):
         far = cross_send[k].at[dr, s]
         product(order[dr][s], rows, rows, columns(k, dr), far)
-        sent["x", k, dr, s] = send(far, cross_recv[k].at[dr, s], across)
+        sent["x", k, dr, s] = send(
+            far, cross_recv[k].at[dr, s], across, ("x", k), 8, cross_send[k]
+        )
 
     def rb(k, s, dr):
         sent["x", k, dr, s].wait_recv()
@@ -399,7 +424,9 @@
         dst = ring_send[k].at[dr, s] if s < 3 else own[k].at[dr]
         product(order[dr][s], 0, rows, columns(k, dr), dst, terms)
         if s < 3:
-            sent["z", k, dr, s] = send(dst, ring_recv[k].at[dr, s], toward[dr])
+            sent["z", k, dr, s] = send(
+                dst, ring_recv[k].at[dr, s], toward[dr], ("z", k), 6, ring_send[k]
+            )
 
     def up(k):
         loaded("states")
@@ -448,8 +475,10 @@
         )
         weight[here] = chosen[k][me]
 
-    def pass_on(at, dev):
-        return send(weight.at[at], weight.at[at], dev)
+    def pass_on(at, dev, k, way, size):
+        count = size // 2 * (block if kinds[k] == "a" and way == "gz" else rows)
+        whole = weight.at[pl.ds(0, count), both(k)]
+        return send(weight.at[at], weight.at[at], dev, (way, k), size, whole)
 
     def md(k):
         sent["move", k].wait_recv()
@@ -457,9 +486,9 @@
         for dr in (0, 1):
             at = (here, columns(k, dr))
             if kinds[k] == "a":
-                sent["gx", k, dr] = pass_on(at, across)
+                sent["gx", k, dr] = pass_on(at, across, k, "gx", 2)
             else:
-                sent["gz", k, dr, 0] = pass_on(at, toward[dr])
+                sent["gz", k, dr, 0] = pass_on(at, toward[dr], k, "gz", 6)
 
     def z_block(s, dr):
         return lax.rem(z + ((4 - s) if dr == 0 else s), 4)
@@ -471,7 +500,9 @@
         else:
             sent["gx", k, dr].wait_recv()
         if s < 3:
-            sent["gz", k, dr, s] = pass_on((pl.ds(row0, block), columns(k, dr)), toward[dr])
+            sent["gz", k, dr, s] = pass_on(
+                (pl.ds(row0, block), columns(k, dr)), toward[dr], k, "gz", 6
+            )
 
     def b_rows(k, s, dr):
         row0 = pl.multiple_of((z_block(s, dr) * 2 + xh) * rows, rows)
@@ -480,10 +511,10 @@
     def gb(k, s, dr):
         sent["gz", k, dr, s - 1].wait_recv()
         if s < 3:
-            sent["gz", k, dr, s] = pass_on(b_rows(k, s, dr), toward[dr])
+            sent["gz", k, dr, s] = pass_on(b_rows(k, s, dr), toward[dr], k, "gz", 6)
 
     def bx(k, s, dr):
-        sent["bx", k, dr, s] = pass_on(b_rows(k, s, dr), across)
+        sent["bx", k, dr, s] = pass_on(b_rows(k, s, dr), across, k, "bx", 8)
 
     def end(k):
         for dr in (0, 1):
@@ -549,7 +580,7 @@
             pltpu.VMEM((3, rows, columns), f32),
             pltpu.SMEM((slots,), jnp.int32),
             pltpu.SemaphoreType.DMA((len(CHUNKS) + 11,)),
-            pltpu.SemaphoreType.DMA((copies,)),
+            pltpu.SemaphoreType.DMA((6 * len(CHUNKS),)),
             pltpu.SemaphoreType.DMA((copies,)),
         ]
         for kind, half in CHUNKS:

time: 107 us -> 106 us (level)
    pallas_call x1, Pallas kernels: 101 us -> 99.9 us  [on_device(): pl.pallas_call(functools.partial(kernel, sizes), out_shape=(state, state,...]
where the time goes in v5:
time: 106 us
  Pallas kernels  104 us (98%)
  between operations  1.45 us (1%)
    pallas_call x1, Pallas kernels, on_device(): pl.pallas_call(functools.partial(kernel, sizes), out_shape=(state, state,...  99.9 us
    pallas_call x1, Pallas kernels, on_device(): pl.pallas_call(keep, out_shape=tuple((jax.ShapeDtypeStruct(r.shape, r.dty...  4.24 us

profile of v5, /device:TPU:0, one launch (start us, length us, event | category | flops | bytes accessed | tf_op | source)
XLA Modules:
  0.0 105.6 jit_solution(8212496296304360070)
XLA Ops:
  1.3 99.9 %step.1 = (f32[256,1536]{1,0:T(8,128)S(1)}, f32[256,1536]{1,0:T(8,128)S(1)}, f32[256,1536]{1,0:T(8,128)S(1)}, bf16[2048,1536]{1,0:T(8,128)(2,1)S(1)}) custom-call(s32[16]{0:T(128)} %old_ref.1, s32[16]{0:T(128)} %new_ref.1, s32[1]{0:T(128)} %bitcast.10.count_ref, bf16[1024,2048]{1,0:T(8,128)(2,1)} %bitcast.11, bf16[1024,1536]{1,0:T(8,128)(2,1)} %bitcast.12, ...), custom_call_target="tpu_custom_call" | custom-call | tf_op jit(solution)/shard_map/step/pallas_call | solution.py:588
  101.2 4.2 %keep.1 = (f32[256,1536]{1,0:T(8,128)}, f32[256,1536]{1,0:T(8,128)}, f32[256,1536]{1,0:T(8,128)}, bf16[2048,1536]{1,0:T(8,128)(2,1)}) custom-call(f32[256,1536]{1,0:T(8,128)S(1)} %get-tuple-element.12.refs_0_, f32[256,1536]{1,0:T(8,128)S(1)} %get-tuple-element.13.refs_1_, f32[256,1536]{1,0:T(8,128)S(1)} %get-tuple-element.14.refs_2_, ...), custom_call_target="tpu_custom_call" | custom-call | tf_op jit(solution)/shard_map/keep/pallas_call | solution.py:608
